TPU v7x, 32 devices: a whole 2x2x4 slice. The times are simulated.
32 devices in a mesh: seq: 4 (over y, core), nbr: 8 (over z, x).
Axes of the slice: x: 2, y: 2, z: 4, core: 2. Of those that a mesh axis runs over, the one named last changes fastest.
Arguments:
- queries: bfloat16 [8192, 2048], P(('seq', 'nbr')), may hold values from -16 to 16
- cotangent: bfloat16 [8192, 2048], P(('seq', 'nbr')), may hold values from -6 to 6
- neighbour_tokens: bfloat16 [256, 128, 896], P(('seq', 'nbr')), may hold values from -6 to 6
- neighbour_ids: int32 [128, 2], P(('seq', 'nbr')), may hold values from 0 to 255, as said below
- neighbour_dest: int32 [256], P(('seq', 'nbr')), may hold values from 0 to 255, as said below
- sequence_ids: int32 [128], P(('seq', 'nbr')), may hold values from 0 to 7, never falling along the last dimension, each value on 1 to 32 neighbouring positions
- enc_in: bfloat16 [896, 1792], replicated, may hold values from -0.1875 to 0.1875
- enc_out: bfloat16 [1792, 896], replicated, may hold values from -0.125 to 0.125
- key_weight: bfloat16 [896, 2048], replicated, may hold values from -0.5 to 0.5
- value_weight: bfloat16 [896, 2048], replicated, may hold values from -0.1875 to 0.1875
Outputs:
- attended: bfloat16 [8192, 2048], P(('seq', 'nbr'))
- grad_encoded: bfloat16 [256, 128, 896], P(('seq', 'nbr'))
Inputs may be any that keep to these rules, and one draw needn't show every extreme that they name: `neighbour_ids`: every number 0 to 255 appears exactly once. Neighbour n is held by device n // 8 in the order seq+nbr, a device of the same seq index as the device holding the span. Among the neighbours of one device's spans at most 2 are held by any one device, and in every draw some device has exactly 2 held by one device. neighbour_dest[neighbour_ids[c, k]] = c * 2 + k for every span c and k.
All inputs are finite; a program needn't handle non-finite values.
Results may differ from a plain program's by a relative error of at most 0.015.
The roundings to bfloat16 on the way count: a program that leaves them out, or rounds other values in their place, can miss the bound.
Values may be sent and summed in bfloat16 or wider, within the bound.
A program may use at most 128 MiB of HBM per device.

v0:
```python
import math

import jax
import jax.numpy as jnp
from jax import lax
from jax.sharding import PartitionSpec as P

HEAD_DIM = 128
CAP = 2


epsilon = 1e-06


def from_behind(block, axis, distance):
    devices = range(lax.axis_size(axis))
    route = [(i - distance, i) for i in devices if i - distance in devices]
    return lax.ppermute(block, axis, route)


def encode(block, enc_in, enc_out):
    inputs = block.astype(jnp.float32)
    scaling = lax.rsqrt(jnp.mean(inputs * inputs, axis=-1, keepdims=True) + epsilon)
    normed = (inputs * scaling).astype(jnp.bfloat16)
    hidden_act = jax.nn.gelu(
        jnp.dot(normed, enc_in, preferred_element_type=jnp.float32), approximate=True
    ).astype(jnp.bfloat16)
    return (inputs + jnp.dot(hidden_act, enc_out, preferred_element_type=jnp.float32)).astype(
        jnp.bfloat16
    )


def attend(query_rows, cot_rows, slot_block, validity, key_weight, value_weight):
    blocks, span_len, features = query_rows.shape
    head_count = features // HEAD_DIM
    slot_count, length, enc_width = slot_block.shape
    flat_slots = slot_block.reshape(slot_count * length, enc_width)
    key_rows = jnp.dot(flat_slots, key_weight, preferred_element_type=jnp.float32).astype(
        jnp.bfloat16
    )
    value_rows = jnp.dot(flat_slots, value_weight, preferred_element_type=jnp.float32).astype(
        jnp.bfloat16
    )
    key_rows = key_rows.reshape(blocks, -1, head_count, HEAD_DIM)
    value_rows = value_rows.reshape(blocks, -1, head_count, HEAD_DIM)
    query_four = query_rows.reshape(blocks, span_len, head_count, HEAD_DIM)
    inv_root = 1.0 / math.sqrt(HEAD_DIM)
    scores = (
        jnp.einsum("cmhd,cphd->chmp", query_four, key_rows, preferred_element_type=jnp.float32)
        * inv_root
    )
    shares = jax.nn.softmax(scores, axis=-1)
    weights = shares.astype(jnp.bfloat16)
    mixture = jnp.einsum("chmp,cphd->cmhd", weights, value_rows, preferred_element_type=jnp.float32)
    attended = (
        (mixture * validity[:, :, None, None])
        .astype(jnp.bfloat16)
        .reshape(blocks, span_len, features)
    )
    masked = (
        cot_rows.reshape(blocks, span_len, head_count, HEAD_DIM)
        * validity.astype(jnp.bfloat16)[:, :, None, None]
    )
    grad_weights = jnp.einsum(
        "cmhd,cphd->chmp", masked, value_rows, preferred_element_type=jnp.float32
    )
    grad_scores = (
        shares * (grad_weights - jnp.sum(shares * grad_weights, axis=-1, keepdims=True))
    ).astype(jnp.bfloat16)
    grad_keys = (
        jnp.einsum("chmp,cmhd->cphd", grad_scores, query_four, preferred_element_type=jnp.float32)
        * inv_root
    ).astype(jnp.bfloat16)
    grad_values = jnp.einsum(
        "chmp,cmhd->cphd", weights, masked, preferred_element_type=jnp.float32
    ).astype(jnp.bfloat16)
    grad_keys = grad_keys.reshape(slot_count * length, features)
    grad_values = grad_values.reshape(slot_count * length, features)
    slot_grads = jnp.dot(grad_keys, key_weight.T, preferred_element_type=jnp.float32) + jnp.dot(
        grad_values, value_weight.T, preferred_element_type=jnp.float32
    )
    return (attended, slot_grads.astype(jnp.bfloat16).reshape(slot_count, length, enc_width))


def shards(
    queries,
    cotangent,
    neighbour_tokens,
    neighbour_ids,
    neighbour_dest,
    sequence_ids,
    enc_in,
    enc_out,
    key_weight,
    value_weight,
):
    span_count = sequence_ids.shape[0]
    token_rows, features = queries.shape
    span_len = token_rows // span_count
    head_rows = span_len - 1
    nb_local, length, enc_width = neighbour_tokens.shape
    peer_count = lax.axis_size("nbr")
    slot_total = peer_count * CAP
    label_send = (sequence_ids[:1] % 128 + 1).astype(jnp.bfloat16)
    next_query, next_cot, next_label = from_behind(
        (queries[:head_rows], cotangent[:head_rows], label_send), ("seq", "nbr"), -1
    )
    own_label = (sequence_ids % 128 + 1).astype(jnp.bfloat16)
    later_label = jnp.concatenate([own_label[1:], next_label], 0)
    offsets = jnp.arange(span_len)
    validity = ((offsets[None, :] == 0) | (own_label[:, None] == later_label[:, None])).astype(
        jnp.float32
    )
    query_ext = jnp.concatenate([queries[head_rows:], next_query], 0).reshape(
        span_count, span_len, features
    )
    cot_ext = jnp.concatenate([cotangent[head_rows:], next_cot], 0).reshape(
        span_count, span_len, features
    )
    encoded = encode(
        neighbour_tokens.reshape(nb_local * length, enc_width), enc_in, enc_out
    ).reshape(nb_local, length, enc_width)
    slot_ids = neighbour_ids.reshape(-1) % (peer_count * nb_local)
    owners = slot_ids // nb_local
    same_owner = (owners[:, None] == owners[None, :]) & (slot_ids[None, :] < slot_ids[:, None])
    recv_slot = owners * CAP + jnp.sum(same_owner.astype(jnp.int32), axis=1)
    dest_peer = neighbour_dest // nb_local % peer_count
    earlier = jnp.arange(nb_local)
    same_dest = (dest_peer[:, None] == dest_peer[None, :]) & (earlier[None, :] < earlier[:, None])
    send_slot = dest_peer * CAP + jnp.sum(same_dest.astype(jnp.int32), axis=1)
    slot_index = jnp.arange(slot_total)
    send_table = (slot_index[:, None] == send_slot[None, :]).astype(jnp.bfloat16)
    outgoing = jnp.dot(
        send_table, encoded.reshape(nb_local, -1), preferred_element_type=jnp.float32
    )
    outgoing = outgoing.astype(jnp.bfloat16).reshape(slot_total, length, enc_width)
    incoming = lax.all_to_all(outgoing, "nbr", split_axis=0, concat_axis=0, tiled=True)
    slot_block = jnp.take(incoming, recv_slot, axis=0)
    attended_ext, slot_grads = attend(
        query_ext, cot_ext, slot_block, validity, key_weight, value_weight
    )
    recv_table = (slot_index[:, None] == recv_slot[None, :]).astype(jnp.bfloat16)
    outgoing_grads = jnp.dot(
        recv_table, slot_grads.reshape(nb_local, -1), preferred_element_type=jnp.float32
    )
    outgoing_grads = outgoing_grads.astype(jnp.bfloat16).reshape(slot_total, length, enc_width)
    returned = lax.all_to_all(outgoing_grads, "nbr", split_axis=0, concat_axis=0, tiled=True)
    grad_encoded = jnp.take(returned, send_slot, axis=0)
    extended = attended_ext.reshape(token_rows, features)
    carried = from_behind(extended[token_rows - head_rows :], ("seq", "nbr"), 1)
    attended = jnp.concatenate([carried, extended[: token_rows - head_rows]], 0)
    return (attended, grad_encoded)


def solution(mesh):
    in_specs = (
        P(("seq", "nbr"), None),
        P(("seq", "nbr"), None),
        P(("seq", "nbr"), None, None),
        P(("seq", "nbr"), None),
        P(("seq", "nbr")),
        P(("seq", "nbr")),
        P(),
        P(),
        P(),
        P(),
    )
    out_specs = (P(("seq", "nbr"), None), P(("seq", "nbr"), None, None))
    return jax.shard_map(shards, mesh=mesh, in_specs=in_specs, out_specs=out_specs, check_vma=False)
```

profile of v0, /device:TPU:17, one launch (start us, length us, event | category | flops | bytes accessed | tf_op | source)
XLA Modules:
  0.0 323.3 jit_solution(5186451390192406818)
XLA Ops:
  0.6 0.0 copy-start
  0.6 0.8 and_select_fusion.3
  1.5 0.2 convert_reduce_fusion.1
  1.7 0.7 compare_and_fusion
  2.3 1.9 fusion.23
  4.3 3.1 fusion.24
  7.4 11.4 %fusion.25 = bf16[1024,896]{1,0:T(8,128)(2,1)} fusion(bf16[8,128,896]{2,1,0:T(8,128)(2,1)} %param.14, bf16[1792,896]{1,0:T(8,128)(2,1)S(1)} %copy-done, bf16[1024,896]{1,0:T(8,128)(2,1)} %fusion.24, bf16[896,1792]{1,0:T(8,128)(2,1)} %param.18), kind=kOutput, calls=%fused_computation.41 | convolution fusion | flops 6595936256 | bytes 11927552 | tf_op jit(solution)/shard_map/dot_general | solution.py:28
  18.8 2.3 reshape_reshape.15
  21.1 1.1 convolution_convert_fusion.1
  22.2 2.5 copy.38
  24.7 5.7 %all-to-all-start = ((bf16[16,128,896]{2,1,0:T(8,128)(2,1)}), bf16[16,128,896]{2,1,0:T(8,128)(2,1)}, u32[]{:S(2)}, u32[]{:S(2)}) async-start(bf16[16,128,896]{2,1,0:T(8,128)(2,1)} %bitcast.66), calls=%async_computation | async-start | bytes 7340032 | tf_op jit(solution)/shard_map/all_to_all | solution.py:137
  30.4 0.0 copy-done.9
  30.6 78.1 %collective-permute-start.1 = (bf16[1]{0:T(256)(128)(2,1)}, bf16[1]{0:T(256)(128)(2,1)}, u32[]{:S(2)}, u32[]{:S(2)}) collective-permute-start(bf16[1]{0:T(256)(128)(2,1)} %convert_element_type.101), channel_id=1, source_target_pairs={{1,0},{2,1},{3,2},{4,3},{5,4},{6,5},{7,6},{8,7},{9,8},{10,9},{11,1... | collective-permute-start | bytes 14 | tf_op jit(solution)/shard_map/ppermute | solution.py:18
  108.6 1.9 collective-permute-start.3
  110.6 2.2 collective-permute-start
  112.8 0.2 slice.24
  113.0 1.1 slice.30
  114.1 0.1 slice.26
  114.2 0.1 copy.27
  114.3 0.1 reshape.220
  114.4 0.2 convert_reduce_fusion
  114.7 0.7 maximum_compare_fusion
  115.4 0.1 fusion.60
  115.4 6.9 %collective-permute-done = bf16[63,2048]{1,0:T(8,128)(2,1)} collective-permute-done((bf16[63,2048]{1,0:T(8,128)(2,1)S(1)}, bf16[63,2048]{1,0:T(8,128)(2,1)}, u32[]{:S(2)}, u32[]{:S(2)}) %collective-permute-start) | collective-permute-done | bytes 258080 | tf_op jit(solution)/shard_map/ppermute | solution.py:18
  122.4 1.1 maximum_bitcast_fusion
  123.5 0.2 copy.37
  123.7 0.0 collective-permute-done.3
  123.7 1.1 maximum_bitcast_fusion.1
  124.8 1.2 copy.42
  126.0 0.0 all-to-all-done
  126.0 2.9 gather_fusion
  128.9 0.2 broadcast_select_fusion.1
  129.2 6.8 %convert_bitcast_fusion.1 = bf16[128,8,16,128]{3,1,2,0:T(8,128)(2,1)S(1)} fusion(bf16[1024,896]{1,0:T(8,128)(2,1)S(1)} %bitcast.79, bf16[896,2048]{1,0:T(8,128)(2,1)} %param.20), kind=kOutput, calls=%fused_computation.28 | convolution fusion | flops 3760193536 | bytes 9699328 | tf_op jit(solution)/shard_map/dot_general | solution.py:38
  136.0 0.0 copy-start.11
  136.0 1.4 copy.39
  137.4 0.6 copy-done.11
  138.1 4.7 %convert_bitcast_fusion.2 = bf16[128,8,16,128]{3,1,2,0:T(8,128)(2,1)S(1)} fusion(bf16[1024,896]{1,0:T(8,128)(2,1)S(1)} %bitcast.80, bf16[896,2048]{1,0:T(8,128)(2,1)S(1)} %copy-done.11), kind=kOutput, calls=%fused_computation.29 | convolution fusion | flops 3760193536 | bytes 9699328 | tf_op jit(solution)/shard_map/dot_general | solution.py:41
  142.8 3.3 %copy.40 = bf16[128,8,16,128]{3,2,1,0:T(8,128)(2,1)} copy(bf16[128,8,16,128]{3,1,2,0:T(8,128)(2,1)S(1)} %convert_bitcast_fusion.2) | data formatting | bytes 8388608
  146.1 1.6 fusion.16
  147.7 0.0 copy-start.8
  147.7 2.9 fusion.73
  150.6 0.3 copy-done.2
  150.9 12.9 %convert_bitcast_fusion = bf16[4,256,16,128]{1,3,2,0:T(8,128)(2,1)} fusion(bf16[4,64,16,128]{3,2,1,0:T(8,128)(2,1)S(1)} %bitcast.81, bf16[4,64]{1,0:T(4,128)(2,1)S(1)} %get-tuple-element.9, f32[4,16,64]{2,1,0:T(8,128)S(1)} %get-tuple-element.11, f32[4,16,64,256]{3,2,1,0:T(8,128)} %copy-done.2), kind=kOutput, calls=%fused_computation.24 | convolution fusion | flops 276304128 | bytes 9454080 | tf_op jit(solution)/shard_map/chmp,cmhd->cphd/dot_general | solution.py:74
  163.7 8.4 %copy.36 = bf16[4,256,16,128]{3,2,1,0:T(8,128)(2,1)} copy(bf16[4,256,16,128]{1,3,2,0:T(8,128)(2,1)} %convert_bitcast_fusion) | data formatting | bytes 8388608 | tf_op jit(solution)/shard_map/convert_element_type | solution.py:76
  172.1 9.8 %fusion.10 = f32[1024,896]{1,0:T(8,128)} fusion(bf16[896,2048]{1,0:T(8,128)(2,1)} %param.21, bf16[128,8,16,128]{3,2,1,0:T(8,128)(2,1)} %bitcast.77), kind=kOutput, calls=%fused_computation.16 | convolution fusion | flops 3758096384 | bytes 11534336 | tf_op jit(solution)/shard_map/dot_general | solution.py:79
  181.9 3.7 %multiply_reduce_fusion = (f32[4,16,64]{2,1,0:T(8,128)S(1)}, f32[4,16,64,256]{3,2,1,0:T(8,128)}) fusion(f32[4,16,64,256]{3,2,1,0:T(8,128)S(1)} %copy-done.4, f32[4,16,64]{2,1,0:T(8,128)S(1)} %get-tuple-element.11, bf16[4,256,16,128]{3,2,1,0:T(8,128)(2,1)S(1)} %bitcast.75, bf16[4,64,16,128]{3,2,1,0:T(8,128)(2,1)S(1)} %bitcast.82, ...), kind=kOutput, calls=%fused_computation.26 | convolution fusion | flops 272101376 | bytes 13664768 | tf_op jit(solution)/shard_map/cmhd,cphd->chmp/dot_general | solution.py:64
  185.7 14.3 %fusion.9 = bf16[4,256,16,128]{1,3,2,0:T(8,128)(2,1)} fusion(f32[4,16,64,256]{3,2,1,0:T(8,128)} %get-tuple-element.14, f32[4,16,64]{2,1,0:T(8,128)S(1)} %get-tuple-element.13, bf16[4,64,16,128]{3,2,1,0:T(8,128)(2,1)S(1)} %bitcast.73, f32[4,16,64]{2,1,0:T(8,128)S(1)} %get-tuple-element.11, f32[4,16,64,256]{3,2,1,0:T(8,128)} %copy-done.2), kind=kOutput, calls=%fused_computation.15 | convolution fusion | flops 279974144 | bytes 13664256 | tf_op jit(solution)/shard_map/chmp,cmhd->cphd/dot_general | solution.py:71
  199.9 8.0 %copy.35 = bf16[4,256,16,128]{3,2,1,0:T(8,128)(2,1)} copy(bf16[4,256,16,128]{1,3,2,0:T(8,128)(2,1)} %fusion.9) | data formatting | bytes 8388608 | tf_op jit(solution)/shard_map/convert_element_type | solution.py:73
  208.0 10.1 %add_convert_fusion = bf16[1024,896]{1,0:T(8,128)(2,1)} fusion(f32[1024,896]{1,0:T(8,128)} %fusion.10, bf16[896,2048]{1,0:T(8,128)(2,1)} %param.20, bf16[128,8,16,128]{3,2,1,0:T(8,128)(2,1)} %bitcast.76), kind=kOutput, calls=%fused_computation.42 | convolution fusion | flops 3759931392 | bytes 13369344 | tf_op jit(solution)/shard_map/dot_general | solution.py:79
  218.1 2.3 reshape_reshape.19
  220.4 1.1 convolution_convert_fusion
  221.5 2.5 copy.45
  224.0 4.7 %all-to-all-start.1 = ((bf16[16,128,896]{2,1,0:T(8,128)(2,1)}), bf16[16,128,896]{2,1,0:T(8,128)(2,1)}, u32[]{:S(2)}, u32[]{:S(2)}) async-start(bf16[16,128,896]{2,1,0:T(8,128)(2,1)} %bitcast.67), calls=%async_computation.1 | async-start | bytes 7340032 | tf_op jit(solution)/shard_map/all_to_all | solution.py:147
  228.7 12.1 %fusion.38 = bf16[4,64,16,128]{3,1,2,0:T(8,128)(2,1)S(1)} fusion(bf16[4,256,16,128]{3,2,1,0:T(8,128)(2,1)} %bitcast.74, f32[4,64]{1,0:T(4,128)S(1)} %get-tuple-element.10, f32[4,16,64]{2,1,0:T(8,128)S(1)} %get-tuple-element.11, f32[4,16,64,256]{3,2,1,0:T(8,128)} %copy-done.2), kind=kOutput, calls=%fused_computation.50 | convolution fusion | flops 274731264 | bytes 9454592 | tf_op jit(solution)/shard_map/chmp,cphd->cmhd/dot_general | solution.py:54
  240.8 0.7 copy.31
  241.4 0.3 copy.78
  241.7 0.1 slice.36
  241.8 2.3 collective-permute-start.2
  244.2 0.1 slice.37
  244.2 70.5 %collective-permute-done.2 = bf16[63,2048]{1,0:T(8,128)(2,1)S(1)} collective-permute-done((bf16[63,2048]{1,0:T(8,128)(2,1)S(1)}, bf16[63,2048]{1,0:T(8,128)(2,1)S(1)}, u32[]{:S(2)}, u32[]{:S(2)}) %collective-permute-start.2) | collective-permute-done | bytes 258080 | tf_op jit(solution)/shard_map/ppermute | solution.py:18
  314.7 1.2 pad_maximum_fusion
  315.9 0.0 all-to-all-done.1
  315.9 4.1 %gather_fusion.1 = bf16[8,128,896]{2,1,0:T(8,128)(2,1)} fusion(bf16[16,128,896]{2,1,0:T(8,128)(2,1)} %all-to-all-done.1, s32[1024]{0:T(1024)S(1)} %pad_clamp_fusion), kind=kCustom, calls=%fused_computation.1.clone | custom fusion | bytes 3670048 | tf_op jit(solution)/shard_map/jit(_take)/gather | solution.py:148
  320.1 3.0 broadcast_select_fusion
  (30 shorter events, 0.1 us)
Async XLA Ops:
  0.6 6.7 %copy-start = (bf16[1792,896]{1,0:T(8,128)(2,1)S(1)}, bf16[1792,896]{1,0:T(8,128)(2,1)}, u32[]{:S(2)}) copy-start(bf16[1792,896]{1,0:T(8,128)(2,1)} %param.19) | copy-start | bytes 9633796
  24.7 5.7 %copy-start.9 = (s32[4]{0:T(128)S(1)}, s32[4]{0:T(128)}, u32[]{:S(2)}) copy-start(s32[4]{0:T(128)} %param.17) | copy-start | bytes 52
  24.7 83.9 %copy-start.7 = (bf16[256,2048]{1,0:T(8,128)(2,1)S(1)}, bf16[256,2048]{1,0:T(8,128)(2,1)}, u32[]{:S(2)}) copy-start(bf16[256,2048]{1,0:T(8,128)(2,1)} %param.13) | copy-start | bytes 3145732
  24.7 85.9 %copy-start.6 = (bf16[256,2048]{1,0:T(8,128)(2,1)S(1)}, bf16[256,2048]{1,0:T(8,128)(2,1)}, u32[]{:S(2)}) copy-start(bf16[256,2048]{1,0:T(8,128)(2,1)} %param.12) | copy-start | bytes 3145732
  24.7 89.5 %copy-start.10 = (s32[4,2]{0,1:T(2,128)S(1)}, s32[4,2]{0,1:T(2,128)}, u32[]{:S(2)}) copy-start(s32[4,2]{0,1:T(2,128)} %param.15) | copy-start | bytes 100
  24.7 101.3 %all-to-all-start = ((bf16[16,128,896]{2,1,0:T(8,128)(2,1)}), bf16[16,128,896]{2,1,0:T(8,128)(2,1)}, u32[]{:S(2)}, u32[]{:S(2)}) async-start(bf16[16,128,896]{2,1,0:T(8,128)(2,1)} %bitcast.66), calls=%async_computation | async-start | bytes 7340032 | tf_op jit(solution)/shard_map/all_to_all | solution.py:137
  30.6 84.1 %collective-permute-start.1 = (bf16[1]{0:T(256)(128)(2,1)}, bf16[1]{0:T(256)(128)(2,1)}, u32[]{:S(2)}, u32[]{:S(2)}) collective-permute-start(bf16[1]{0:T(256)(128)(2,1)} %convert_element_type.101), channel_id=1, source_target_pairs={{1,0},{2,1},{3,2},{4,3},{5,4},{6,5},{7,6},{8,7},{9,8},{10,9},{11,1... | collective-permute-start | bytes 14 | tf_op jit(solution)/shard_map/ppermute | solution.py:18
  108.6 15.0 %collective-permute-start.3 = (bf16[63,2048]{1,0:T(8,128)(2,1)S(1)}, bf16[63,2048]{1,0:T(8,128)(2,1)}, u32[]{:S(2)}, u32[]{:S(2)}) collective-permute-start(bf16[63,2048]{1,0:T(8,128)(2,1)S(1)} %slice.31), channel_id=1, source_target_pairs={{1,0},{2,1},{3,2},{4,3},{5,4},{6,5},{7,6},{8,7},{9,8},{10,9},{11,1... | collective-permute-start | bytes 774152 | tf_op jit(solution)/shard_map/ppermute | solution.py:18
  110.6 11.7 %collective-permute-start = (bf16[63,2048]{1,0:T(8,128)(2,1)S(1)}, bf16[63,2048]{1,0:T(8,128)(2,1)}, u32[]{:S(2)}, u32[]{:S(2)}) collective-permute-start(bf16[63,2048]{1,0:T(8,128)(2,1)S(1)} %slice.25), channel_id=1, source_target_pairs={{1,0},{2,1},{3,2},{4,3},{5,4},{6,5},{7,6},{8,7},{9,8},{10,9},{11,1... | collective-permute-start | bytes 774152 | tf_op jit(solution)/shard_map/ppermute | solution.py:18
  114.4 9.3 %copy-start.5 = (bf16[193,2048]{1,0:T(8,128)(2,1)S(1)}, bf16[193,2048]{1,0:T(8,128)(2,1)}, u32[]{:S(2)}) copy-start(bf16[193,2048]{1,0:T(8,128)(2,1)} %slice.30) | copy-start | bytes 2371588
  136.0 2.0 copy-start.11
  147.7 3.2 copy-start.2
  147.7 3.2 copy-start.8
  172.1 9.8 %copy-start.3 = (bf16[128,8,16,128]{3,2,1,0:T(8,128)(2,1)S(1)}, bf16[128,8,16,128]{3,2,1,0:T(8,128)(2,1)}, u32[]{:S(2)}) copy-start(bf16[128,8,16,128]{3,2,1,0:T(8,128)(2,1)} %copy.40) | copy-start | bytes 12582916
  172.1 9.8 %copy-start.4 = (f32[4,16,64,256]{3,2,1,0:T(8,128)S(1)}, f32[4,16,64,256]{3,2,1,0:T(8,128)}, u32[]{:S(2)}) copy-start(f32[4,16,64,256]{3,2,1,0:T(8,128)} %get-tuple-element.12) | copy-start | bytes 12582916
  224.0 91.9 %all-to-all-start.1 = ((bf16[16,128,896]{2,1,0:T(8,128)(2,1)}), bf16[16,128,896]{2,1,0:T(8,128)(2,1)}, u32[]{:S(2)}, u32[]{:S(2)}) async-start(bf16[16,128,896]{2,1,0:T(8,128)(2,1)} %bitcast.67), calls=%async_computation.1 | async-start | bytes 7340032 | tf_op jit(solution)/shard_map/all_to_all | solution.py:147
  241.8 72.9 %collective-permute-start.2 = (bf16[63,2048]{1,0:T(8,128)(2,1)S(1)}, bf16[63,2048]{1,0:T(8,128)(2,1)S(1)}, u32[]{:S(2)}, u32[]{:S(2)}) collective-permute-start(bf16[63,2048]{1,0:T(8,128)(2,1)S(1)} %slice.36), channel_id=1, source_target_pairs={{0,1},{1,2},{2,3},{3,4},{4,5},{5,6},{6,7},{7,8},{8,9},{9,10},{10,1... | collective-permute-start | bytes 774152 | tf_op jit(solution)/shard_map/ppermute | solution.py:18
  314.7 8.3 %copy-start.1 = (bf16[1792,896]{1,0:T(8,128)(2,1)S(1)}, bf16[1792,896]{1,0:T(8,128)(2,1)}, u32[]{:S(2)}) copy-start(bf16[1792,896]{1,0:T(8,128)(2,1)} %param.19) | copy-start | bytes 9633796
where the time goes:
time: 330 us; the launch traced here: 323 us
  starting transfers between devices  94.9 us (29%)
  matrix products  89.5 us (27%)
  waiting for transfers between devices  77.4 us (23%)
  local copies, waits for them, and re-layouts  42.9 us (13%)
  other arithmetic  17.2 us (5%)
    ppermute x4, starting transfers between devices, from_behind(): return lax.ppermute(block, axis, route)  84.5 us
    ppermute x4, waiting for transfers between devices, from_behind(): return lax.ppermute(block, axis, route)  77.4 us
    dot_general x1, matrix products, attend(): jnp.einsum('chmp,cmhd->cphd', grad_scores, query_four, preferred_element_...  14.3 us
    dot_general x1, matrix products, attend(): jnp.einsum('chmp,cmhd->cphd', weights, masked, preferred_element_type=jnp...  12.9 us
    unnamed x32, local copies, waits for them, and re-layouts  12.5 us
    dot_general x1, matrix products, attend(): jnp.einsum('chmp,cphd->cmhd', weights, value_rows, preferred_element_type...  12.1 us
    dot_general x1, matrix products, encode(): jnp.dot(hidden_act, enc_out, preferred_element_type=jnp.float32)  11.4 us
    dot_general x1, matrix products, attend(): jnp.dot(grad_keys, key_weight.T, preferred_element_type=jnp.float32)  10.1 us
  transfers between devices with their start and end apart: 6, of which 2 were waited for; matrix products, arithmetic and copies ran while one was open for 6% of the time, Pallas kernels for 0%

commit v1 on v0

v1 whole, which is shorter than its diff:
```python
import functools
import math

import jax
import jax.numpy as jnp
from jax import lax
from jax.experimental import pallas as pl
from jax.experimental.pallas import tpu as pltpu
from jax.sharding import PartitionSpec as P

HEAD_DIM = 128
CAP = 2
CHUNK = 256
PARTS = 2


epsilon = 1e-06

NT = (((1,), (1,)), ((), ()))
TN = (((0,), (0,)), ((), ()))


def from_behind(block, axis, distance):
    devices = range(lax.axis_size(axis))
    route = [(i - distance, i) for i in devices if i - distance in devices]
    return lax.ppermute(block, axis, route)


def dot(a, b, dims=(((1,), (0,)), ((), ()))):
    return lax.dot_general(a, b, dims, preferred_element_type=jnp.float32)


def encode_kernel(slot_ref, x_ref, in_ref, out_w_ref, out_ref, normed, acc):
    step = pl.program_id(0)
    count, rows, width = x_ref.shape

    @pl.when(step == 0)
    def _():
        inputs = x_ref[...].reshape(count * rows, width).astype(jnp.float32)
        scaling = lax.rsqrt(jnp.mean(inputs * inputs, axis=-1, keepdims=True) + epsilon)
        normed[...] = (inputs * scaling).astype(jnp.bfloat16)
        acc[...] = inputs

    hidden = jax.nn.gelu(dot(normed[...], in_ref[...]), approximate=True).astype(jnp.bfloat16)
    acc[...] += dot(hidden, out_w_ref[...])

    @pl.when(step == pl.num_programs(0) - 1)
    def _():
        for n in range(count):
            out_ref[slot_ref[n]] = acc[n * rows : (n + 1) * rows].astype(jnp.bfloat16)


def encode_part(part, tokens, enc_in, enc_out, send_slot, slot_total):
    count, length, width = tokens.shape
    rows = length // PARTS
    hidden = enc_in.shape[1]
    return pl.pallas_call(
        encode_kernel,
        grid_spec=pltpu.PrefetchScalarGridSpec(
            num_scalar_prefetch=1,
            grid=(hidden // CHUNK,),
            in_specs=[
                pl.BlockSpec((count, rows, width), lambda j, s: (0, part, 0)),
                pl.BlockSpec((width, CHUNK), lambda j, s: (0, j)),
                pl.BlockSpec((CHUNK, width), lambda j, s: (j, 0)),
            ],
            out_specs=pl.BlockSpec((slot_total, rows, width), lambda j, s: (0, 0, 0)),
            scratch_shapes=[
                pltpu.VMEM((count * rows, width), jnp.bfloat16),
                pltpu.VMEM((count * rows, width), jnp.float32),
            ],
        ),
        out_shape=jax.ShapeDtypeStruct((slot_total, rows, width), jnp.bfloat16),
        cost_estimate=pl.CostEstimate(
            flops=4 * count * rows * width * hidden,
            bytes_accessed=4 * width * hidden + 6 * count * rows * width,
            transcendentals=count * rows * hidden,
        ),
        name="encode_part",
    )(send_slot, tokens, enc_in, enc_out)


def gather_rows(slot_ref, x_ref, held, slots):
    rows = x_ref.shape[1]
    for n in range(slots):
        held[n * rows : (n + 1) * rows] = x_ref[slot_ref[n]]


def project_kernel(slots, slot_ref, x_ref, kw_ref, vw_ref, k_ref, v_ref, held):
    @pl.when(pl.program_id(0) == 0)
    def _():
        gather_rows(slot_ref, x_ref, held, slots)

    k_ref[...] = dot(held[...], kw_ref[...]).astype(jnp.bfloat16)
    v_ref[...] = dot(held[...], vw_ref[...]).astype(jnp.bfloat16)


def project_part(incoming, key_weight, value_weight, recv_slot):
    slot_total, rows, width = incoming.shape
    slots = recv_slot.shape[0]
    features = key_weight.shape[1]
    wide = 2 * CHUNK
    weight = pl.BlockSpec((width, wide), lambda j, s: (0, j))
    result = pl.BlockSpec((slots * rows, wide), lambda j, s: (0, j))
    shape = jax.ShapeDtypeStruct((slots * rows, features), jnp.bfloat16)
    return pl.pallas_call(
        functools.partial(project_kernel, slots),
        grid_spec=pltpu.PrefetchScalarGridSpec(
            num_scalar_prefetch=1,
            grid=(features // wide,),
            in_specs=[
                pl.BlockSpec((slot_total, rows, width), lambda j, s: (0, 0, 0)),
                weight,
                weight,
            ],
            out_specs=[result, result],
            scratch_shapes=[pltpu.VMEM((slots * rows, width), jnp.bfloat16)],
        ),
        out_shape=[shape, shape],
        cost_estimate=pl.CostEstimate(
            flops=4 * slots * rows * width * features,
            bytes_accessed=4 * width * features + 4 * slots * rows * features,
            transcendentals=0,
        ),
        name="project_part",
    )(recv_slot, incoming, key_weight, value_weight)


def attend_kernel(
    slots, spans, slot_ref, x_ref, ka_ref, va_ref, kw_ref, vw_ref, q_ref, c_ref, valid_ref,
    out_ref, gka_ref, gva_ref, gkb_ref, gvb_ref, held,
):
    @pl.when(pl.program_id(0) == 0)
    def _():
        gather_rows(slot_ref, x_ref, held, slots)

    inv_root = 1.0 / math.sqrt(HEAD_DIM)
    kb = dot(held[...], kw_ref[...]).astype(jnp.bfloat16)
    vb = dot(held[...], vw_ref[...]).astype(jnp.bfloat16)
    half = held.shape[0] // spans
    tokens = q_ref.shape[0] // spans
    for c in range(spans):
        near = slice(c * half, (c + 1) * half)
        mine = slice(c * tokens, (c + 1) * tokens)
        valid = valid_ref[mine]
        for h in range(q_ref.shape[1] // HEAD_DIM):
            cols = slice(h * HEAD_DIM, (h + 1) * HEAD_DIM)
            keys = jnp.concatenate([ka_ref[near, cols], kb[near, cols]], 0)
            values = jnp.concatenate([va_ref[near, cols], vb[near, cols]], 0)
            query = q_ref[mine, cols]
            masked = (c_ref[mine, cols].astype(jnp.float32) * valid).astype(jnp.bfloat16)
            scores = dot(query, keys, NT) * inv_root
            powers = jnp.exp(scores - jnp.max(scores, axis=-1, keepdims=True))
            shares = powers / jnp.sum(powers, axis=-1, keepdims=True)
            weights = shares.astype(jnp.bfloat16)
            out_ref[mine, cols] = (dot(weights, values) * valid).astype(jnp.bfloat16)
            grad_weights = dot(masked, values, NT)
            inner = jnp.sum(shares * grad_weights, axis=-1, keepdims=True)
            grad_scores = (shares * (grad_weights - inner)).astype(jnp.bfloat16)
            grad_keys = (dot(grad_scores, query, TN) * inv_root).astype(jnp.bfloat16)
            grad_values = dot(weights, masked, TN).astype(jnp.bfloat16)
            gka_ref[near, cols] = grad_keys[:half]
            gkb_ref[near, cols] = grad_keys[half:]
            gva_ref[near, cols] = grad_values[:half]
            gvb_ref[near, cols] = grad_values[half:]


def attend_all(incoming, keys_a, values_a, key_weight, value_weight, query, cot, valid, recv_slot):
    slot_total, rows, width = incoming.shape
    slots = recv_slot.shape[0]
    tokens, features = query.shape
    spans = valid.shape[0]
    column = valid.reshape(tokens, 1)
    weight = pl.BlockSpec((width, CHUNK), lambda j, s: (0, j))
    near = pl.BlockSpec((slots * rows, CHUNK), lambda j, s: (0, j))
    mine = pl.BlockSpec((tokens, CHUNK), lambda j, s: (0, j))
    shape = jax.ShapeDtypeStruct((slots * rows, features), jnp.bfloat16)
    positions = PARTS * slots * rows // spans
    return pl.pallas_call(
        functools.partial(attend_kernel, slots, spans),
        grid_spec=pltpu.PrefetchScalarGridSpec(
            num_scalar_prefetch=1,
            grid=(features // CHUNK,),
            in_specs=[
                pl.BlockSpec((slot_total, rows, width), lambda j, s: (0, 0, 0)),
                near,
                near,
                weight,
                weight,
                mine,
                mine,
                pl.BlockSpec((tokens, 1), lambda j, s: (0, 0)),
            ],
            out_specs=[mine, near, near, near, near],
            scratch_shapes=[pltpu.VMEM((slots * rows, width), jnp.bfloat16)],
        ),
        out_shape=[jax.ShapeDtypeStruct((tokens, features), jnp.bfloat16)] + [shape] * 4,
        cost_estimate=pl.CostEstimate(
            flops=4 * slots * rows * width * features + 10 * tokens * positions * features,
            bytes_accessed=4 * width * features + 12 * slots * rows * features,
            transcendentals=tokens * positions * features // HEAD_DIM,
        ),
        name="attend_all",
    )(recv_slot, incoming, keys_a, values_a, key_weight, value_weight, query, cot, column)


def return_kernel(slots, slot_ref, gk_ref, gv_ref, kw_ref, vw_ref, out_ref, acc):
    step = pl.program_id(0)

    @pl.when(step == 0)
    def _():
        acc[...] = jnp.zeros_like(acc)

    acc[...] += dot(gk_ref[...], kw_ref[...], NT) + dot(gv_ref[...], vw_ref[...], NT)

    @pl.when(step == pl.num_programs(0) - 1)
    def _():
        rows = out_ref.shape[1]
        for n in range(slots):
            out_ref[slot_ref[n]] = acc[n * rows : (n + 1) * rows].astype(jnp.bfloat16)


def return_part(grad_keys, grad_values, key_weight, value_weight, recv_slot, slot_total):
    slots = recv_slot.shape[0]
    total_rows, features = grad_keys.shape
    rows = total_rows // slots
    width = key_weight.shape[0]
    wide = 2 * CHUNK
    weight = pl.BlockSpec((width, wide), lambda j, s: (0, j))
    near = pl.BlockSpec((total_rows, wide), lambda j, s: (0, j))
    return pl.pallas_call(
        functools.partial(return_kernel, slots),
        grid_spec=pltpu.PrefetchScalarGridSpec(
            num_scalar_prefetch=1,
            grid=(features // wide,),
            in_specs=[near, near, weight, weight],
            out_specs=pl.BlockSpec((slot_total, rows, width), lambda j, s: (0, 0, 0)),
            scratch_shapes=[pltpu.VMEM((total_rows, width), jnp.float32)],
        ),
        out_shape=jax.ShapeDtypeStruct((slot_total, rows, width), jnp.bfloat16),
        cost_estimate=pl.CostEstimate(
            flops=4 * total_rows * width * features,
            bytes_accessed=4 * width * features + 4 * total_rows * features,
            transcendentals=0,
        ),
        name="return_part",
    )(recv_slot, grad_keys, grad_values, key_weight, value_weight)


def place_kernel(slot_ref, first_ref, second_ref, out_ref):
    rows = first_ref.shape[1]
    out_ref[0, :rows] = first_ref[0]
    out_ref[0, rows:] = second_ref[0]


def place(first, second, send_slot):
    _, rows, width = first.shape
    count = send_slot.shape[0]
    chosen = pl.BlockSpec((1, rows, width), lambda n, s: (s[n], 0, 0))
    return pl.pallas_call(
        place_kernel,
        grid_spec=pltpu.PrefetchScalarGridSpec(
            num_scalar_prefetch=1,
            grid=(count,),
            in_specs=[chosen, chosen],
            out_specs=pl.BlockSpec((1, PARTS * rows, width), lambda n, s: (n, 0, 0)),
        ),
        out_shape=jax.ShapeDtypeStruct((count, PARTS * rows, width), jnp.bfloat16),
        name="place",
    )(send_slot, first, second)


def exchange(block):
    return lax.all_to_all(block, "nbr", split_axis=0, concat_axis=0, tiled=True)


def shards(
    queries,
    cotangent,
    neighbour_tokens,
    neighbour_ids,
    neighbour_dest,
    sequence_ids,
    enc_in,
    enc_out,
    key_weight,
    value_weight,
):
    span_count = sequence_ids.shape[0]
    token_rows, features = queries.shape
    span_len = token_rows // span_count
    head_rows = span_len - 1
    nb_local = neighbour_tokens.shape[0]
    peer_count = lax.axis_size("nbr")
    slot_total = peer_count * CAP

    dest_peer = neighbour_dest // nb_local % peer_count
    earlier = jnp.arange(nb_local)
    same_dest = (dest_peer[:, None] == dest_peer[None, :]) & (earlier[None, :] < earlier[:, None])
    send_slot = dest_peer * CAP + jnp.sum(same_dest.astype(jnp.int32), axis=1)
    slot_ids = neighbour_ids.reshape(-1) % (peer_count * nb_local)
    owners = slot_ids // nb_local
    same_owner = (owners[:, None] == owners[None, :]) & (slot_ids[None, :] < slot_ids[:, None])
    recv_slot = owners * CAP + jnp.sum(same_owner.astype(jnp.int32), axis=1)

    sent_a = encode_part(0, neighbour_tokens, enc_in, enc_out, send_slot, slot_total)
    in_a = exchange(sent_a)
    sent_b = encode_part(1, neighbour_tokens, enc_in, enc_out, send_slot, slot_total)
    in_b = exchange(sent_b)

    label_send = (sequence_ids[:1] % 128 + 1).astype(jnp.bfloat16)
    next_query, next_cot, next_label = from_behind(
        (queries[:head_rows], cotangent[:head_rows], label_send), ("seq", "nbr"), -1
    )
    own_label = (sequence_ids % 128 + 1).astype(jnp.bfloat16)
    later_label = jnp.concatenate([own_label[1:], next_label], 0)
    offsets = jnp.arange(span_len)
    validity = ((offsets[None, :] == 0) | (own_label[:, None] == later_label[:, None])).astype(
        jnp.float32
    )
    query_ext = jnp.concatenate([queries[head_rows:], next_query], 0)
    cot_ext = jnp.concatenate([cotangent[head_rows:], next_cot], 0)

    keys_a, values_a = project_part(in_a, key_weight, value_weight, recv_slot)
    extended, gka, gva, gkb, gvb = attend_all(
        in_b, keys_a, values_a, key_weight, value_weight, query_ext, cot_ext, validity, recv_slot
    )
    back_a = exchange(return_part(gka, gva, key_weight, value_weight, recv_slot, slot_total))
    back_b = exchange(return_part(gkb, gvb, key_weight, value_weight, recv_slot, slot_total))
    carried = from_behind(extended[token_rows - head_rows :], ("seq", "nbr"), 1)
    attended = jnp.concatenate([carried, extended[: token_rows - head_rows]], 0)
    return (attended, place(back_a, back_b, send_slot))


def solution(mesh):
    in_specs = (
        P(("seq", "nbr"), None),
        P(("seq", "nbr"), None),
        P(("seq", "nbr"), None, None),
        P(("seq", "nbr"), None),
        P(("seq", "nbr")),
        P(("seq", "nbr")),
        P(),
        P(),
        P(),
        P(),
    )
    out_specs = (P(("seq", "nbr"), None), P(("seq", "nbr"), None, None))
    return jax.shard_map(shards, mesh=mesh, in_specs=in_specs, out_specs=out_specs, check_vma=False)
```

time: 330 us -> 294 us (0.89); the launches traced: 323 us -> 293 us
  Pallas kernels: 0 us -> 101 us
  matrix products: 89.5 us -> 0 us
  local copies, waits for them, and re-layouts: 42.9 us -> 8.57 us
  waiting for transfers between devices: 77.4 us -> 103 us
  starting transfers between devices: 94.9 us -> 71.6 us
  other arithmetic: 17.2 us -> 8.9 us
    pallas_call x0 -> x7, Pallas kernels: none -> 101 us  [the longest x1 40 us: attend_all(): pl.pallas_call(functools.partial(attend_kernel, slots, spans), grid_spec=...]
    dot_general x12 -> x0, matrix products: 89.5 us -> none  [the longest x1 14.3 us: attend(): jnp.einsum('chmp,cmhd->cphd', grad_scores, query_four, preferred_element_...]
    all_to_all x2 -> x4, waiting for transfers between devices: 0.01 us -> 53.9 us  [exchange(): return lax.all_to_all(block, 'nbr', split_axis=0, concat_axis=0, tiled=True)]
    ppermute x4, starting transfers between devices: 84.5 us -> 45.8 us  [from_behind(): return lax.ppermute(block, axis, route)]
    ppermute x4, waiting for transfers between devices: 77.4 us -> 48.7 us  [from_behind(): return lax.ppermute(block, axis, route)]
    convert_element_type x3 -> x1, local copies, waits for them, and re-layouts: 17.1 us -> 0.8 us  [shards(): ((offsets[None, :] == 0) | (own_label[:, None] == later_label[:, None]))....]
    all_to_all x2 -> x4, starting transfers between devices: 10.4 us -> 25.8 us  [exchange(): return lax.all_to_all(block, 'nbr', split_axis=0, concat_axis=0, tiled=True)]
    unnamed x32 -> x15, local copies, waits for them, and re-layouts: 12.5 us -> 2.6 us
  transfers between devices with their start and end apart: 6 -> 8, of which waited for: 2 -> 4; matrix products, arithmetic and copies ran while one was open for 6% -> 4% of each run, Pallas kernels for 0% -> 11%
where the time goes in v1:
time: 294 us; the launch traced here: 293 us
  waiting for transfers between devices  103 us (35%)
  Pallas kernels  101 us (34%)
  starting transfers between devices  71.6 us (24%)
  other arithmetic  8.9 us (3%)
  local copies, waits for them, and re-layouts  8.57 us (3%)
    all_to_all x4, waiting for transfers between devices, exchange(): return lax.all_to_all(block, 'nbr', split_axis=0, concat_axis=0, tiled=True)  53.9 us
    ppermute x4, waiting for transfers between devices, from_behind(): return lax.ppermute(block, axis, route)  48.7 us
    ppermute x4, starting transfers between devices, from_behind(): return lax.ppermute(block, axis, route)  45.8 us
    pallas_call x1, Pallas kernels, attend_all(): pl.pallas_call(functools.partial(attend_kernel, slots, spans), grid_spec=...  40 us
    all_to_all x4, starting transfers between devices, exchange(): return lax.all_to_all(block, 'nbr', split_axis=0, concat_axis=0, tiled=True)  25.8 us
    pallas_call x2, Pallas kernels, encode_part(): pl.pallas_call(encode_kernel, grid_spec=pltpu.PrefetchScalarGridSpec(num_...  25.5 us
    pallas_call x2, Pallas kernels, return_part(): pl.pallas_call(functools.partial(return_kernel, slots), grid_spec=pltpu.P...  19.4 us
    pallas_call x1, Pallas kernels, project_part(): pl.pallas_call(functools.partial(project_kernel, slots), grid_spec=pltpu....  9.54 us
  transfers between devices with their start and end apart: 8, of which 4 were waited for; matrix products, arithmetic and copies ran while one was open for 4% of the time, Pallas kernels for 11%

profile of v1, /device:TPU:17, one launch (start us, length us, event | category | flops | bytes accessed | tf_op | source)
XLA Modules:
  0.0 293.2 jit_solution(9329851691721160102)
XLA Ops:
  0.6 0.7 and_select_fusion.1
  1.3 0.2 convert_reduce_fusion
  1.5 1.2 multiply_add_fusion.slot_ref
  2.7 12.7 %encode_part.3 = bf16[16,64,896]{2,1,0:T(8,128)(2,1)} custom-call(s32[8]{0:T(128)} %multiply_add_fusion.slot_ref, bf16[8,128,896]{2,1,0:T(8,128)(2,1)} %x_ref.3, bf16[896,1792]{1,0:T(8,128)(2,1)} %in_ref.3, bf16[1792,896]{1,0:T(8,128)(2,1)} %out_w_ref.3), custom_call_target="tpu_custom_call" | custom-call | flops 3288334336 | bytes 9175040 | tf_op jit(solution)/shard_map/encode_part/pallas_call | solution.py:57
  15.5 5.6 %all-to-all-start.1 = ((bf16[16,64,896]{2,1,0:T(8,128)(2,1)}), bf16[16,64,896]{2,1,0:T(8,128)(2,1)S(1)}, u32[]{:S(2)}, u32[]{:S(2)}) async-start(bf16[16,64,896]{2,1,0:T(8,128)(2,1)} %encode_part.3), calls=%async_computation.1 | async-start | bytes 3670016 | tf_op jit(solution)/shard_map/all_to_all | solution.py:274
  21.1 12.7 %encode_part.2 = bf16[16,64,896]{2,1,0:T(8,128)(2,1)} custom-call(s32[8]{0:T(128)} %multiply_add_fusion.slot_ref, bf16[8,128,896]{2,1,0:T(8,128)(2,1)} %x_ref.3, bf16[896,1792]{1,0:T(8,128)(2,1)} %in_ref.3, bf16[1792,896]{1,0:T(8,128)(2,1)} %out_w_ref.3), custom_call_target="tpu_custom_call" | custom-call | flops 3288334336 | bytes 9175040 | tf_op jit(solution)/shard_map/encode_part/pallas_call | solution.py:57
  33.8 0.0 copy-start.5
  33.8 26.1 %all-to-all-done.1.x_ref = bf16[16,64,896]{2,1,0:T(8,128)(2,1)S(1)} async-done(((bf16[16,64,896]{2,1,0:T(8,128)(2,1)}), bf16[16,64,896]{2,1,0:T(8,128)(2,1)S(1)}, u32[]{:S(2)}, u32[]{:S(2)}) %all-to-all-start.1) | async-done | bytes 1835040 | tf_op jit(solution)/shard_map/all_to_all | solution.py:274
  59.9 0.0 copy-start.2
  59.9 1.3 copy-done.2
  61.1 7.6 %all-to-all-start = ((bf16[16,64,896]{2,1,0:T(8,128)(2,1)}), bf16[16,64,896]{2,1,0:T(8,128)(2,1)S(1)}, u32[]{:S(2)}, u32[]{:S(2)}) async-start(bf16[16,64,896]{2,1,0:T(8,128)(2,1)} %encode_part.2), calls=%async_computation | async-start | bytes 3670016 | tf_op jit(solution)/shard_map/all_to_all | solution.py:274
  68.8 0.0 copy-start.3
  68.8 0.0 copy-done.5
  68.9 0.0 copy-start.6
  68.9 38.9 %collective-permute-start.2 = (bf16[1]{0:T(256)(128)(2,1)}, bf16[1]{0:T(256)(128)(2,1)}, u32[]{:S(2)}, u32[]{:S(2)}) collective-permute-start(bf16[1]{0:T(256)(128)(2,1)} %convert_element_type.28), channel_id=1, source_target_pairs={{1,0},{2,1},{3,2},{4,3},{5,4},{6,5},{7,6},{8,7},{9,8},{10,9},{11,1... | collective-permute-start | bytes 14 | tf_op jit(solution)/shard_map/ppermute | solution.py:26
  107.8 1.7 slice.27
  109.5 1.9 collective-permute-start.1
  111.4 1.7 slice.25
  113.1 1.9 collective-permute-start
  115.0 1.3 slice.24
  116.3 0.0 copy-done.3
  116.3 0.2 slice.26
  116.6 0.1 slice.28
  116.6 0.0 copy-done.6
  116.6 0.1 copy.15
  116.7 0.1 reshape.132
  116.8 0.2 convert_reduce_fusion.1
  117.0 0.5 multiply_add_fusion.1.slot_ref
  117.6 0.0 collective-permute-done.2
  117.6 0.7 maximum_compare_fusion
  118.3 0.1 or_convert_fusion
  118.3 0.8 reshape.134.valid_ref
  119.1 4.5 %collective-permute-done = bf16[63,2048]{1,0:T(8,128)(2,1)} collective-permute-done((bf16[63,2048]{1,0:T(8,128)(2,1)}, bf16[63,2048]{1,0:T(8,128)(2,1)}, u32[]{:S(2)}, u32[]{:S(2)}) %collective-permute-start) | collective-permute-done | bytes 258080 | tf_op jit(solution)/shard_map/ppermute | solution.py:26
  123.6 2.0 pad_maximum_fusion.q_ref
  125.6 0.0 collective-permute-done.1
  125.6 2.0 pad_maximum_fusion.1.c_ref
  127.7 9.5 %project_part.1 = (bf16[512,2048]{1,0:T(8,128)(2,1)}, bf16[512,2048]{1,0:T(8,128)(2,1)}) custom-call(s32[8]{0:T(128)} %multiply_add_fusion.1.slot_ref, bf16[16,64,896]{2,1,0:T(8,128)(2,1)} %copy-done.2, bf16[896,2048]{1,0:T(8,128)(2,1)} %kw_ref.7, bf16[896,2048]{1,0:T(8,128)(2,1)} %vw_ref.7), custom_call_target="tpu_custom_call" | custom-call | flops 3758096384 | bytes 11534336 | tf_op jit(solution)/shard_map/project_part/pallas_call | solution.py:106
  137.2 0.0 all-to-all-done.x_ref
  137.2 0.0 copy-start.1
  137.2 1.2 copy-done.1
  138.4 40.0 %attend_all.1 = (bf16[256,2048]{1,0:T(8,128)(2,1)}, bf16[512,2048]{1,0:T(8,128)(2,1)}, bf16[512,2048]{1,0:T(8,128)(2,1)}, bf16[512,2048]{1,0:T(8,128)(2,1)}, bf16[512,2048]{1,0:T(8,128)(2,1)}) custom-call(s32[8]{0:T(128)} %multiply_add_fusion.1.slot_ref, bf16[16,64,896]{2,1,0:T(8,128)(2,1)} %copy-done.1, bf16[512,2048]{1,0:T(8,128)(2,1)} %get-tuple-element.9.ka_ref, ...), custom_call_target="tpu_custom_call" | custom-call | flops 5100273664 | bytes 19922944 | tf_op jit(solution)/shard_map/attend_all/pallas_call | solution.py:179
  178.4 9.7 %return_part.3 = bf16[16,64,896]{2,1,0:T(8,128)(2,1)} custom-call(s32[8]{0:T(128)} %multiply_add_fusion.1.slot_ref, bf16[512,2048]{1,0:T(8,128)(2,1)} %get-tuple-element.14.gk_ref, bf16[512,2048]{1,0:T(8,128)(2,1)} %get-tuple-element.15.gv_ref, bf16[896,2048]{1,0:T(8,128)(2,1)} %kw_ref.7, bf16[896,2048]{1,0:T(8,128)(2,1)} %vw_ref.7), custom_call_target="tpu_custom_call" | custom-call | flops 3758096384 | bytes 11534336 | tf_op jit(solution)/shard_map/return_part/pallas_call | solution.py:231
  188.2 3.6 %all-to-all-start.3 = ((bf16[16,64,896]{2,1,0:T(8,128)(2,1)}), bf16[16,64,896]{2,1,0:T(8,128)(2,1)S(1)}, u32[]{:S(2)}, u32[]{:S(2)}) async-start(bf16[16,64,896]{2,1,0:T(8,128)(2,1)} %return_part.3), calls=%async_computation.3 | async-start | bytes 3670016 | tf_op jit(solution)/shard_map/all_to_all | solution.py:274
  191.8 9.7 %return_part.2 = bf16[16,64,896]{2,1,0:T(8,128)(2,1)} custom-call(s32[8]{0:T(128)} %multiply_add_fusion.1.slot_ref, bf16[512,2048]{1,0:T(8,128)(2,1)} %get-tuple-element.12.gk_ref, bf16[512,2048]{1,0:T(8,128)(2,1)} %get-tuple-element.13.gv_ref, bf16[896,2048]{1,0:T(8,128)(2,1)} %kw_ref.7, bf16[896,2048]{1,0:T(8,128)(2,1)} %vw_ref.7), custom_call_target="tpu_custom_call" | custom-call | flops 3758096384 | bytes 11534336 | tf_op jit(solution)/shard_map/return_part/pallas_call | solution.py:231
  201.5 0.0 copy-start.4
  201.5 27.8 %all-to-all-done.3.second_ref = bf16[16,64,896]{2,1,0:T(8,128)(2,1)S(1)} async-done(((bf16[16,64,896]{2,1,0:T(8,128)(2,1)}), bf16[16,64,896]{2,1,0:T(8,128)(2,1)S(1)}, u32[]{:S(2)}, u32[]{:S(2)}) %all-to-all-start.3) | async-done | bytes 1835040 | tf_op jit(solution)/shard_map/all_to_all | solution.py:274
  229.3 0.0 copy-start
  229.3 8.9 %all-to-all-start.2 = ((bf16[16,64,896]{2,1,0:T(8,128)(2,1)}), bf16[16,64,896]{2,1,0:T(8,128)(2,1)}, u32[]{:S(2)}, u32[]{:S(2)}) async-start(bf16[16,64,896]{2,1,0:T(8,128)(2,1)} %return_part.2), calls=%async_computation.2 | async-start | bytes 3670016 | tf_op jit(solution)/shard_map/all_to_all | solution.py:274
  238.2 0.0 copy-done.4
  238.2 0.1 slice.30
  238.3 0.0 copy-done
  238.3 3.1 %collective-permute-start.3 = (bf16[63,2048]{1,0:T(8,128)(2,1)S(1)}, bf16[63,2048]{1,0:T(8,128)(2,1)S(1)}, u32[]{:S(2)}, u32[]{:S(2)}) collective-permute-start(bf16[63,2048]{1,0:T(8,128)(2,1)S(1)} %slice.30), channel_id=1, source_target_pairs={{0,1},{1,2},{2,3},{3,4},{4,5},{5,6},{6,7},{7,8},{8,9},{9,10},{10,1... | collective-permute-start | bytes 774152 | tf_op jit(solution)/shard_map/ppermute | solution.py:26
  241.4 0.1 slice.31
  241.4 44.3 %collective-permute-done.3 = bf16[63,2048]{1,0:T(8,128)(2,1)S(1)} collective-permute-done((bf16[63,2048]{1,0:T(8,128)(2,1)S(1)}, bf16[63,2048]{1,0:T(8,128)(2,1)S(1)}, u32[]{:S(2)}, u32[]{:S(2)}) %collective-permute-start.3) | collective-permute-done | bytes 258080 | tf_op jit(solution)/shard_map/ppermute | solution.py:26
  285.7 1.2 pad_maximum_fusion.2
  286.9 0.0 all-to-all-done.2.first_ref
  286.9 6.3 %place.1 = bf16[8,128,896]{2,1,0:T(8,128)(2,1)} custom-call(s32[8]{0:T(128)} %multiply_add_fusion.slot_ref, bf16[16,64,896]{2,1,0:T(8,128)(2,1)} %all-to-all-done.2.first_ref, bf16[16,64,896]{2,1,0:T(8,128)(2,1)} %copy-done), custom_call_target="tpu_custom_call" | custom-call | tf_op jit(solution)/shard_map/place/pallas_call | solution.py:260
  (3 shorter events, 0.0 us)
Async XLA Ops:
  15.5 44.4 %all-to-all-start.1 = ((bf16[16,64,896]{2,1,0:T(8,128)(2,1)}), bf16[16,64,896]{2,1,0:T(8,128)(2,1)S(1)}, u32[]{:S(2)}, u32[]{:S(2)}) async-start(bf16[16,64,896]{2,1,0:T(8,128)(2,1)} %encode_part.3), calls=%async_computation.1 | async-start | bytes 3670016 | tf_op jit(solution)/shard_map/all_to_all | solution.py:274
  33.8 35.0 %copy-start.5 = (s32[4]{0:T(128)S(1)}, s32[4]{0:T(128)}, u32[]{:S(2)}) copy-start(s32[4]{0:T(128)} %param.15) | copy-start | bytes 52
  59.9 1.3 copy-start.2
  61.1 76.1 %all-to-all-start = ((bf16[16,64,896]{2,1,0:T(8,128)(2,1)}), bf16[16,64,896]{2,1,0:T(8,128)(2,1)S(1)}, u32[]{:S(2)}, u32[]{:S(2)}) async-start(bf16[16,64,896]{2,1,0:T(8,128)(2,1)} %encode_part.2), calls=%async_computation | async-start | bytes 3670016 | tf_op jit(solution)/shard_map/all_to_all | solution.py:274
  68.8 47.6 %copy-start.3 = (bf16[256,2048]{1,0:T(8,128)(2,1)S(1)}, bf16[256,2048]{1,0:T(8,128)(2,1)}, u32[]{:S(2)}) copy-start(bf16[256,2048]{1,0:T(8,128)(2,1)} %param.11) | copy-start | bytes 3145732
  68.9 47.8 %copy-start.6 = (s32[4,2]{0,1:T(2,128)S(1)}, s32[4,2]{0,1:T(2,128)}, u32[]{:S(2)}) copy-start(s32[4,2]{0,1:T(2,128)} %param.13) | copy-start | bytes 100
  68.9 48.7 %collective-permute-start.2 = (bf16[1]{0:T(256)(128)(2,1)}, bf16[1]{0:T(256)(128)(2,1)}, u32[]{:S(2)}, u32[]{:S(2)}) collective-permute-start(bf16[1]{0:T(256)(128)(2,1)} %convert_element_type.28), channel_id=1, source_target_pairs={{1,0},{2,1},{3,2},{4,3},{5,4},{6,5},{7,6},{8,7},{9,8},{10,9},{11,1... | collective-permute-start | bytes 14 | tf_op jit(solution)/shard_map/ppermute | solution.py:26
  109.5 16.2 %collective-permute-start.1 = (bf16[63,2048]{1,0:T(8,128)(2,1)}, bf16[63,2048]{1,0:T(8,128)(2,1)}, u32[]{:S(2)}, u32[]{:S(2)}) collective-permute-start(bf16[63,2048]{1,0:T(8,128)(2,1)} %slice.27), channel_id=1, source_target_pairs={{1,0},{2,1},{3,2},{4,3},{5,4},{6,5},{7,6},{8,7},{9,8},{10,9},{11,1... | collective-permute-start | bytes 774152 | tf_op jit(solution)/shard_map/ppermute | solution.py:26
  113.1 10.5 %collective-permute-start = (bf16[63,2048]{1,0:T(8,128)(2,1)}, bf16[63,2048]{1,0:T(8,128)(2,1)}, u32[]{:S(2)}, u32[]{:S(2)}) collective-permute-start(bf16[63,2048]{1,0:T(8,128)(2,1)} %slice.25), channel_id=1, source_target_pairs={{1,0},{2,1},{3,2},{4,3},{5,4},{6,5},{7,6},{8,7},{9,8},{10,9},{11,1... | collective-permute-start | bytes 774152 | tf_op jit(solution)/shard_map/ppermute | solution.py:26
  137.2 1.2 copy-start.1
  188.2 41.1 %all-to-all-start.3 = ((bf16[16,64,896]{2,1,0:T(8,128)(2,1)}), bf16[16,64,896]{2,1,0:T(8,128)(2,1)S(1)}, u32[]{:S(2)}, u32[]{:S(2)}) async-start(bf16[16,64,896]{2,1,0:T(8,128)(2,1)} %return_part.3), calls=%async_computation.3 | async-start | bytes 3670016 | tf_op jit(solution)/shard_map/all_to_all | solution.py:274
  201.5 36.7 %copy-start.4 = (bf16[256,2048]{1,0:T(8,128)(2,1)S(1)}, bf16[256,2048]{1,0:T(8,128)(2,1)}, u32[]{:S(2)}) copy-start(bf16[256,2048]{1,0:T(8,128)(2,1)} %get-tuple-element.11) | copy-start | bytes 3145732
  229.3 9.0 %copy-start = (bf16[16,64,896]{2,1,0:T(8,128)(2,1)}, bf16[16,64,896]{2,1,0:T(8,128)(2,1)S(1)}, u32[]{:S(2)}) copy-start(bf16[16,64,896]{2,1,0:T(8,128)(2,1)S(1)} %all-to-all-done.3.second_ref) | copy-start | bytes 5505028
  229.3 57.7 %all-to-all-start.2 = ((bf16[16,64,896]{2,1,0:T(8,128)(2,1)}), bf16[16,64,896]{2,1,0:T(8,128)(2,1)}, u32[]{:S(2)}, u32[]{:S(2)}) async-start(bf16[16,64,896]{2,1,0:T(8,128)(2,1)} %return_part.2), calls=%async_computation.2 | async-start | bytes 3670016 | tf_op jit(solution)/shard_map/all_to_all | solution.py:274
  238.3 47.4 %collective-permute-start.3 = (bf16[63,2048]{1,0:T(8,128)(2,1)S(1)}, bf16[63,2048]{1,0:T(8,128)(2,1)S(1)}, u32[]{:S(2)}, u32[]{:S(2)}) collective-permute-start(bf16[63,2048]{1,0:T(8,128)(2,1)S(1)} %slice.30), channel_id=1, source_target_pairs={{0,1},{1,2},{2,3},{3,4},{4,5},{5,6},{6,7},{7,8},{8,9},{9,10},{10,1... | collective-permute-start | bytes 774152 | tf_op jit(solution)/shard_map/ppermute | solution.py:26

commit v2 on v1

--- a/solution.py
+++ b/solution.py
@@ -54,15 +54,16 @@
     count, length, width = tokens.shape
     rows = length // PARTS
     hidden = enc_in.shape[1]
+    wide = hidden // 2
     return pl.pallas_call(
         encode_kernel,
         grid_spec=pltpu.PrefetchScalarGridSpec(
             num_scalar_prefetch=1,
-            grid=(hidden // CHUNK,),
+            grid=(hidden // wide,),
             in_specs=[
                 pl.BlockSpec((count, rows, width), lambda j, s: (0, part, 0)),
-                pl.BlockSpec((width, CHUNK), lambda j, s: (0, j)),
-                pl.BlockSpec((CHUNK, width), lambda j, s: (j, 0)),
+                pl.BlockSpec((width, wide), lambda j, s: (0, j)),
+                pl.BlockSpec((wide, width), lambda j, s: (j, 0)),
             ],
             out_specs=pl.BlockSpec((slot_total, rows, width), lambda j, s: (0, 0, 0)),
             scratch_shapes=[
@@ -139,30 +140,39 @@
     vb = dot(held[...], vw_ref[...]).astype(jnp.bfloat16)
     half = held.shape[0] // spans
     tokens = q_ref.shape[0] // spans
-    for c in range(spans):
-        near = slice(c * half, (c + 1) * half)
-        mine = slice(c * tokens, (c + 1) * tokens)
-        valid = valid_ref[mine]
-        for h in range(q_ref.shape[1] // HEAD_DIM):
-            cols = slice(h * HEAD_DIM, (h + 1) * HEAD_DIM)
-            keys = jnp.concatenate([ka_ref[near, cols], kb[near, cols]], 0)
-            values = jnp.concatenate([va_ref[near, cols], vb[near, cols]], 0)
-            query = q_ref[mine, cols]
-            masked = (c_ref[mine, cols].astype(jnp.float32) * valid).astype(jnp.bfloat16)
-            scores = dot(query, keys, NT) * inv_root
-            powers = jnp.exp(scores - jnp.max(scores, axis=-1, keepdims=True))
-            shares = powers / jnp.sum(powers, axis=-1, keepdims=True)
-            weights = shares.astype(jnp.bfloat16)
-            out_ref[mine, cols] = (dot(weights, values) * valid).astype(jnp.bfloat16)
-            grad_weights = dot(masked, values, NT)
-            inner = jnp.sum(shares * grad_weights, axis=-1, keepdims=True)
-            grad_scores = (shares * (grad_weights - inner)).astype(jnp.bfloat16)
-            grad_keys = (dot(grad_scores, query, TN) * inv_root).astype(jnp.bfloat16)
-            grad_values = dot(weights, masked, TN).astype(jnp.bfloat16)
-            gka_ref[near, cols] = grad_keys[:half]
-            gkb_ref[near, cols] = grad_keys[half:]
-            gva_ref[near, cols] = grad_values[:half]
-            gvb_ref[near, cols] = grad_values[half:]
+    units = [
+        (
+            slice(c * half, (c + 1) * half),
+            slice(c * tokens, (c + 1) * tokens),
+            slice(h * HEAD_DIM, (h + 1) * HEAD_DIM),
+        )
+        for c in range(spans)
+        for h in range(q_ref.shape[1] // HEAD_DIM)
+    ]
+    keys = [jnp.concatenate([ka_ref[n, f], kb[n, f]], 0) for n, _, f in units]
+    values = [jnp.concatenate([va_ref[n, f], vb[n, f]], 0) for n, _, f in units]
+    masked = [
+        (c_ref[m, f].astype(jnp.float32) * valid_ref[m]).astype(jnp.bfloat16) for _, m, f in units
+    ]
+    scores = [dot(q_ref[m, f], k, NT) * inv_root for (_, m, f), k in zip(units, keys)]
+    grad_weights = [dot(g, v, NT) for g, v in zip(masked, values)]
+    powers = [jnp.exp(x - jnp.max(x, axis=-1, keepdims=True)) for x in scores]
+    shares = [x * (1.0 / jnp.sum(x, axis=-1, keepdims=True)) for x in powers]
+    weights = [x.astype(jnp.bfloat16) for x in shares]
+    grad_scores = [
+        (x * (g - jnp.sum(x * g, axis=-1, keepdims=True))).astype(jnp.bfloat16)
+        for x, g in zip(shares, grad_weights)
+    ]
+    for (_, m, f), w, v in zip(units, weights, values):
+        out_ref[m, f] = (dot(w, v) * valid_ref[m]).astype(jnp.bfloat16)
+    for (n, _, f), w, g in zip(units, weights, masked):
+        grad_values = dot(w, g, TN).astype(jnp.bfloat16)
+        gva_ref[n, f] = grad_values[:half]
+        gvb_ref[n, f] = grad_values[half:]
+    for (n, m, f), g in zip(units, grad_scores):
+        grad_keys = (dot(g, q_ref[m, f], TN) * inv_root).astype(jnp.bfloat16)
+        gka_ref[n, f] = grad_keys[:half]
+        gkb_ref[n, f] = grad_keys[half:]
 
 
 def attend_all(incoming, keys_a, values_a, key_weight, value_weight, query, cot, valid, recv_slot):
@@ -225,7 +235,7 @@
     total_rows, features = grad_keys.shape
     rows = total_rows // slots
     width = key_weight.shape[0]
-    wide = 2 * CHUNK
+    wide = features // 2
     weight = pl.BlockSpec((width, wide), lambda j, s: (0, j))
     near = pl.BlockSpec((total_rows, wide), lambda j, s: (0, j))
     return pl.pallas_call(
@@ -247,27 +257,29 @@
     )(recv_slot, grad_keys, grad_values, key_weight, value_weight)
 
 
-def place_kernel(slot_ref, first_ref, second_ref, out_ref):
-    rows = first_ref.shape[1]
-    out_ref[0, :rows] = first_ref[0]
-    out_ref[0, rows:] = second_ref[0]
-
-
-def place(first, second, send_slot):
-    _, rows, width = first.shape
+def place_kernel(slot_ref, x_ref, *refs):
+    out_ref = refs[-1]
+    for n in range(out_ref.shape[0]):
+        out_ref[n] = x_ref[slot_ref[n]]
+
+
+def place(part, returned, send_slot, partial):
+    slot_total, rows, width = returned.shape
     count = send_slot.shape[0]
-    chosen = pl.BlockSpec((1, rows, width), lambda n, s: (s[n], 0, 0))
+    whole = [] if partial is None else [partial]
     return pl.pallas_call(
         place_kernel,
         grid_spec=pltpu.PrefetchScalarGridSpec(
             num_scalar_prefetch=1,
-            grid=(count,),
-            in_specs=[chosen, chosen],
-            out_specs=pl.BlockSpec((1, PARTS * rows, width), lambda n, s: (n, 0, 0)),
+            grid=(1,),
+            in_specs=[pl.BlockSpec((slot_total, rows, width), lambda n, s: (0, 0, 0))]
+            + [pl.BlockSpec(memory_space=pl.ANY)] * len(whole),
+            out_specs=pl.BlockSpec((count, rows, width), lambda n, s: (0, part, 0)),
         ),
         out_shape=jax.ShapeDtypeStruct((count, PARTS * rows, width), jnp.bfloat16),
+        input_output_aliases={2: 0} if whole else {},
         name="place",
-    )(send_slot, first, second)
+    )(send_slot, returned, *whole)
 
 
 def exchange(block):
@@ -303,15 +315,17 @@
     same_owner = (owners[:, None] == owners[None, :]) & (slot_ids[None, :] < slot_ids[:, None])
     recv_slot = owners * CAP + jnp.sum(same_owner.astype(jnp.int32), axis=1)
 
+    label_send = (sequence_ids[:1] % 128 + 1).astype(jnp.bfloat16)
+    next_query, next_cot, next_label = from_behind(
+        (queries[:head_rows], cotangent[:head_rows], label_send), ("seq", "nbr"), -1
+    )
     sent_a = encode_part(0, neighbour_tokens, enc_in, enc_out, send_slot, slot_total)
+    sent_a, next_query, next_cot, next_label = lax.optimization_barrier(
+        (sent_a, next_query, next_cot, next_label)
+    )
     in_a = exchange(sent_a)
     sent_b = encode_part(1, neighbour_tokens, enc_in, enc_out, send_slot, slot_total)
     in_b = exchange(sent_b)
-
-    label_send = (sequence_ids[:1] % 128 + 1).astype(jnp.bfloat16)
-    next_query, next_cot, next_label = from_behind(
-        (queries[:head_rows], cotangent[:head_rows], label_send), ("seq", "nbr"), -1
-    )
     own_label = (sequence_ids % 128 + 1).astype(jnp.bfloat16)
     later_label = jnp.concatenate([own_label[1:], next_label], 0)
     offsets = jnp.arange(span_len)
@@ -325,11 +339,16 @@
     extended, gka, gva, gkb, gvb = attend_all(
         in_b, keys_a, values_a, key_weight, value_weight, query_ext, cot_ext, validity, recv_slot
     )
-    back_a = exchange(return_part(gka, gva, key_weight, value_weight, recv_slot, slot_total))
-    back_b = exchange(return_part(gkb, gvb, key_weight, value_weight, recv_slot, slot_total))
     carried = from_behind(extended[token_rows - head_rows :], ("seq", "nbr"), 1)
+    grads_a = return_part(gka, gva, key_weight, value_weight, recv_slot, slot_total)
+    grads_a, carried = lax.optimization_barrier((grads_a, carried))
+    back_a = exchange(grads_a)
+    grads_b = return_part(gkb, gvb, key_weight, value_weight, recv_slot, slot_total)
+    back_a, grads_b = lax.optimization_barrier((back_a, grads_b))
+    back_b = exchange(grads_b)
     attended = jnp.concatenate([carried, extended[: token_rows - head_rows]], 0)
-    return (attended, place(back_a, back_b, send_slot))
+    grad_encoded = place(1, back_b, send_slot, place(0, back_a, send_slot, None))
+    return (attended, grad_encoded)
 
 
 def solution(mesh):

time: 294 us -> 259 us (0.88)
  the two profiles are of different devices: /device:TPU:17 before, /device:TPU:0 now
where the time goes in v2:
time: 259 us; the launch traced here: 258 us
  waiting for transfers between devices  134 us (52%)
  Pallas kernels  72.1 us (28%)
  starting transfers between devices  31.1 us (12%)
  local copies, waits for them, and re-layouts  9.98 us (4%)
  other arithmetic  7.51 us (3%)
  between operations  2.72 us (1%)
    all_to_all x4, waiting for transfers between devices, exchange(): return lax.all_to_all(block, 'nbr', split_axis=0, concat_axis=0, tiled=True)  133 us
    all_to_all x4, starting transfers between devices, exchange(): return lax.all_to_all(block, 'nbr', split_axis=0, concat_axis=0, tiled=True)  23.8 us
    pallas_call x2, Pallas kernels, return_part(): pl.pallas_call(functools.partial(return_kernel, slots), grid_spec=pltpu.P...  19.2 us
    pallas_call x1, Pallas kernels, attend_all(): pl.pallas_call(functools.partial(attend_kernel, slots, spans), grid_spec=...  19 us
    pallas_call x2, Pallas kernels, encode_part(): pl.pallas_call(encode_kernel, grid_spec=pltpu.PrefetchScalarGridSpec(num_...  18.1 us
    pallas_call x1, Pallas kernels, project_part(): pl.pallas_call(functools.partial(project_kernel, slots), grid_spec=pltpu....  9.54 us
    ppermute x4, starting transfers between devices, from_behind(): return lax.ppermute(block, axis, route)  7.27 us
    pallas_call x2, Pallas kernels, place(): pl.pallas_call(place_kernel, grid_spec=pltpu.PrefetchScalarGridSpec(num_s...  6.3 us
  transfers between devices with their start and end apart: 8, of which 5 were waited for; matrix products, arithmetic and copies ran while one was open for 5% of the time, Pallas kernels for 19%

profile of v2, /device:TPU:0, one launch (start us, length us, event | category | flops | bytes accessed | tf_op | source)
XLA Modules:
  0.0 257.7 jit_solution(5295909000019997822)
XLA Ops:
  2.6 1.3 collective-permute-start.2
  3.9 1.0 slice.25
  4.9 1.3 collective-permute-start.1
  6.2 1.0 slice.24
  7.1 1.3 collective-permute-start
  8.4 0.7 and_select_fusion.1
  9.1 0.2 convert_reduce_fusion
  9.3 1.2 multiply_add_fusion.slot_ref
  10.5 9.0 %encode_part.3 = bf16[16,64,896]{2,1,0:T(8,128)(2,1)} custom-call(s32[8]{0:T(128)} %multiply_add_fusion.slot_ref, bf16[8,128,896]{2,1,0:T(8,128)(2,1)} %x_ref.3, bf16[896,1792]{1,0:T(8,128)(2,1)} %in_ref.3, bf16[1792,896]{1,0:T(8,128)(2,1)} %out_w_ref.3), custom_call_target="tpu_custom_call" | custom-call | flops 3288334336 | bytes 9175040 | tf_op jit(solution)/shard_map/encode_part/pallas_call | solution.py:58
  19.5 0.0 collective-permute-done.2
  19.5 0.0 collective-permute-done.1
  19.6 0.0 copy-start.4
  19.6 1.4 collective-permute-done
  21.0 0.0 copy-start.5
  21.0 0.0 copy-done.4
  21.0 0.7 copy-done.5
  21.7 11.5 %all-to-all-start.1 = ((bf16[16,64,896]{2,1,0:T(8,128)(2,1)}), bf16[16,64,896]{2,1,0:T(8,128)(2,1)S(1)}, u32[]{:S(2)}, u32[]{:S(2)}) async-start(bf16[16,64,896]{2,1,0:T(8,128)(2,1)} %encode_part.3), calls=%async_computation.1 | async-start | bytes 3670016 | tf_op jit(solution)/shard_map/all_to_all | solution.py:286
  33.2 9.0 %encode_part.2 = bf16[16,64,896]{2,1,0:T(8,128)(2,1)} custom-call(s32[8]{0:T(128)} %multiply_add_fusion.slot_ref, bf16[8,128,896]{2,1,0:T(8,128)(2,1)} %x_ref.3, bf16[896,1792]{1,0:T(8,128)(2,1)} %in_ref.3, bf16[1792,896]{1,0:T(8,128)(2,1)} %out_w_ref.3), custom_call_target="tpu_custom_call" | custom-call | flops 3288334336 | bytes 9175040 | tf_op jit(solution)/shard_map/encode_part/pallas_call | solution.py:58
  42.2 34.6 %all-to-all-done.1.x_ref = bf16[16,64,896]{2,1,0:T(8,128)(2,1)S(1)} async-done(((bf16[16,64,896]{2,1,0:T(8,128)(2,1)}), bf16[16,64,896]{2,1,0:T(8,128)(2,1)S(1)}, u32[]{:S(2)}, u32[]{:S(2)}) %all-to-all-start.1) | async-done | bytes 1835040 | tf_op jit(solution)/shard_map/all_to_all | solution.py:286
  76.8 0.0 copy-start.2
  76.8 1.3 copy-done.2
  78.1 4.0 %all-to-all-start = ((bf16[16,64,896]{2,1,0:T(8,128)(2,1)}), bf16[16,64,896]{2,1,0:T(8,128)(2,1)S(1)}, u32[]{:S(2)}, u32[]{:S(2)}) async-start(bf16[16,64,896]{2,1,0:T(8,128)(2,1)} %encode_part.2), calls=%async_computation | async-start | bytes 3670016 | tf_op jit(solution)/shard_map/all_to_all | solution.py:286
  82.1 0.0 copy-start.6
  82.1 0.0 copy-start.7
  82.1 1.4 slice.27
  83.4 1.3 slice.28
  84.8 0.0 copy-done.6
  84.8 0.1 slice.29
  84.9 0.0 copy-done.7
  84.9 0.1 copy.16
  85.0 0.1 reshape.132
  85.1 0.2 convert_reduce_fusion.1
  85.3 0.6 multiply_add_fusion.1.slot_ref
  85.9 0.7 maximum_compare_fusion
  86.6 0.1 or_convert_fusion
  86.7 0.8 reshape.134.valid_ref
  87.5 2.6 %pad_maximum_fusion = (bf16[256,2048]{1,0:T(8,128)(2,1)}, bf16[256,2048]{1,0:T(8,128)(2,1)}) fusion(bf16[63,2048]{1,0:T(8,128)(2,1)} %copy-done.5, bf16[193,2048]{1,0:T(8,128)(2,1)S(1)} %slice.27, bf16[63,2048]{1,0:T(8,128)(2,1)} %copy-done.4, bf16[193,2048]{1,0:T(8,128)(2,1)S(1)} %slice.28), kind=kLoop, calls=%fused_computation | loop fusion | flops 4194304 | bytes 4194304 | tf_op jit(solution)/shard_map/concatenate | solution.py:335
  90.1 9.5 %project_part.1 = (bf16[512,2048]{1,0:T(8,128)(2,1)}, bf16[512,2048]{1,0:T(8,128)(2,1)}) custom-call(s32[8]{0:T(128)} %multiply_add_fusion.1.slot_ref, bf16[16,64,896]{2,1,0:T(8,128)(2,1)} %copy-done.2, bf16[896,2048]{1,0:T(8,128)(2,1)} %kw_ref.7, bf16[896,2048]{1,0:T(8,128)(2,1)} %vw_ref.7), custom_call_target="tpu_custom_call" | custom-call | flops 3758096384 | bytes 11534336 | tf_op jit(solution)/shard_map/project_part/pallas_call | solution.py:107
  99.6 25.7 %all-to-all-done.x_ref = bf16[16,64,896]{2,1,0:T(8,128)(2,1)S(1)} async-done(((bf16[16,64,896]{2,1,0:T(8,128)(2,1)}), bf16[16,64,896]{2,1,0:T(8,128)(2,1)S(1)}, u32[]{:S(2)}, u32[]{:S(2)}) %all-to-all-start) | async-done | bytes 1835040 | tf_op jit(solution)/shard_map/all_to_all | solution.py:286
  125.3 0.0 copy-start.1
  125.3 1.2 copy-done.1
  126.5 19.0 %attend_all.1 = (bf16[256,2048]{1,0:T(8,128)(2,1)}, bf16[512,2048]{1,0:T(8,128)(2,1)}, bf16[512,2048]{1,0:T(8,128)(2,1)}, bf16[512,2048]{1,0:T(8,128)(2,1)}, bf16[512,2048]{1,0:T(8,128)(2,1)}) custom-call(s32[8]{0:T(128)} %multiply_add_fusion.1.slot_ref, bf16[16,64,896]{2,1,0:T(8,128)(2,1)} %copy-done.1, bf16[512,2048]{1,0:T(8,128)(2,1)} %get-tuple-element.18.ka_ref, ...), custom_call_target="tpu_custom_call" | custom-call | flops 5100273664 | bytes 19922944 | tf_op jit(solution)/shard_map/attend_all/pallas_call | solution.py:189
  145.5 1.0 slice.30
  146.5 3.4 %collective-permute-start.3 = (bf16[63,2048]{1,0:T(8,128)(2,1)S(1)}, bf16[63,2048]{1,0:T(8,128)(2,1)S(1)}, u32[]{:S(2)}, u32[]{:S(2)}) collective-permute-start(bf16[63,2048]{1,0:T(8,128)(2,1)S(1)} %slice.30), channel_id=1, source_target_pairs={{0,1},{1,2},{2,3},{3,4},{4,5},{5,6},{6,7},{7,8},{8,9},{9,10},{10,1... | collective-permute-start | bytes 774152 | tf_op jit(solution)/shard_map/ppermute | solution.py:26
  149.9 9.6 %return_part.2 = bf16[16,64,896]{2,1,0:T(8,128)(2,1)} custom-call(s32[8]{0:T(128)} %multiply_add_fusion.1.slot_ref, bf16[512,2048]{1,0:T(8,128)(2,1)} %get-tuple-element.23.gk_ref, bf16[512,2048]{1,0:T(8,128)(2,1)} %get-tuple-element.24.gv_ref, bf16[896,2048]{1,0:T(8,128)(2,1)} %kw_ref.7, bf16[896,2048]{1,0:T(8,128)(2,1)} %vw_ref.7), custom_call_target="tpu_custom_call" | custom-call | flops 3758096384 | bytes 11534336 | tf_op jit(solution)/shard_map/return_part/pallas_call | solution.py:241
  159.5 0.0 collective-permute-done.3
  159.5 3.8 %all-to-all-start.2 = ((bf16[16,64,896]{2,1,0:T(8,128)(2,1)}), bf16[16,64,896]{2,1,0:T(8,128)(2,1)S(1)}, u32[]{:S(2)}, u32[]{:S(2)}) async-start(bf16[16,64,896]{2,1,0:T(8,128)(2,1)} %return_part.2), calls=%async_computation.2 | async-start | bytes 3670016 | tf_op jit(solution)/shard_map/all_to_all | solution.py:286
  163.3 9.6 %return_part.3 = bf16[16,64,896]{2,1,0:T(8,128)(2,1)} custom-call(s32[8]{0:T(128)} %multiply_add_fusion.1.slot_ref, bf16[512,2048]{1,0:T(8,128)(2,1)} %get-tuple-element.28.gk_ref, bf16[512,2048]{1,0:T(8,128)(2,1)} %get-tuple-element.29.gv_ref, bf16[896,2048]{1,0:T(8,128)(2,1)} %kw_ref.7, bf16[896,2048]{1,0:T(8,128)(2,1)} %vw_ref.7), custom_call_target="tpu_custom_call" | custom-call | flops 3758096384 | bytes 11534336 | tf_op jit(solution)/shard_map/return_part/pallas_call | solution.py:241
  172.9 0.0 copy-start.3
  172.9 33.2 %all-to-all-done.2.x_ref = bf16[16,64,896]{2,1,0:T(8,128)(2,1)S(1)} async-done(((bf16[16,64,896]{2,1,0:T(8,128)(2,1)}), bf16[16,64,896]{2,1,0:T(8,128)(2,1)S(1)}, u32[]{:S(2)}, u32[]{:S(2)}) %all-to-all-start.2) | async-done | bytes 1835040 | tf_op jit(solution)/shard_map/all_to_all | solution.py:286
  206.1 0.0 copy-start
  206.1 4.5 %all-to-all-start.3 = ((bf16[16,64,896]{2,1,0:T(8,128)(2,1)}), bf16[16,64,896]{2,1,0:T(8,128)(2,1)}, u32[]{:S(2)}, u32[]{:S(2)}) async-start(bf16[16,64,896]{2,1,0:T(8,128)(2,1)} %return_part.3), calls=%async_computation.3 | async-start | bytes 3670016 | tf_op jit(solution)/shard_map/all_to_all | solution.py:286
  210.6 0.0 copy-done.3
  210.7 0.1 slice.31
  210.7 0.0 copy-done
  210.7 1.2 pad_maximum_fusion.2
  211.9 3.1 %place.2.refs_0_ = bf16[8,128,896]{2,1,0:T(8,128)(2,1)} custom-call(s32[8]{0:T(128)} %multiply_add_fusion.slot_ref, bf16[16,64,896]{2,1,0:T(8,128)(2,1)} %copy-done), custom_call_target="tpu_custom_call" | custom-call | tf_op jit(solution)/shard_map/place/pallas_call | solution.py:270
  215.1 39.5 %all-to-all-done.3.x_ref = bf16[16,64,896]{2,1,0:T(8,128)(2,1)} async-done(((bf16[16,64,896]{2,1,0:T(8,128)(2,1)}), bf16[16,64,896]{2,1,0:T(8,128)(2,1)}, u32[]{:S(2)}, u32[]{:S(2)}) %all-to-all-start.3) | async-done | bytes 1835040 | tf_op jit(solution)/shard_map/all_to_all | solution.py:286
  254.6 3.2 %place.3 = bf16[8,128,896]{2,1,0:T(8,128)(2,1)} custom-call(s32[8]{0:T(128)} %multiply_add_fusion.slot_ref, bf16[16,64,896]{2,1,0:T(8,128)(2,1)} %all-to-all-done.3.x_ref, bf16[8,128,896]{2,1,0:T(8,128)(2,1)} %place.2.refs_0_), custom_call_target="tpu_custom_call", output_to_operand_aliasing={{}: (2, {})} | custom-call | tf_op jit(solution)/shard_map/place/pallas_call | solution.py:270
  (3 shorter events, 0.0 us)
Async XLA Ops:
  2.6 17.0 %collective-permute-start.2 = (bf16[1]{0:T(256)(128)(2,1)}, bf16[1]{0:T(256)(128)(2,1)}, u32[]{:S(2)}, u32[]{:S(2)}) collective-permute-start(bf16[1]{0:T(256)(128)(2,1)} %convert_element_type.27), channel_id=1, source_target_pairs={{1,0},{2,1},{3,2},{4,3},{5,4},{6,5},{7,6},{8,7},{9,8},{10,9},{11,1... | collective-permute-start | bytes 14 | tf_op jit(solution)/shard_map/ppermute | solution.py:26
  4.9 14.7 %collective-permute-start.1 = (bf16[63,2048]{1,0:T(8,128)(2,1)S(1)}, bf16[63,2048]{1,0:T(8,128)(2,1)S(1)}, u32[]{:S(2)}, u32[]{:S(2)}) collective-permute-start(bf16[63,2048]{1,0:T(8,128)(2,1)S(1)} %slice.25), channel_id=1, source_target_pairs={{1,0},{2,1},{3,2},{4,3},{5,4},{6,5},{7,6},{8,7},{9,8},{10,9},{11,1... | collective-permute-start | bytes 774152 | tf_op jit(solution)/shard_map/ppermute | solution.py:26
  7.1 13.8 %collective-permute-start = (bf16[63,2048]{1,0:T(8,128)(2,1)S(1)}, bf16[63,2048]{1,0:T(8,128)(2,1)S(1)}, u32[]{:S(2)}, u32[]{:S(2)}) collective-permute-start(bf16[63,2048]{1,0:T(8,128)(2,1)S(1)} %slice.24), channel_id=1, source_target_pairs={{1,0},{2,1},{3,2},{4,3},{5,4},{6,5},{7,6},{8,7},{9,8},{10,9},{11,1... | collective-permute-start | bytes 774152 | tf_op jit(solution)/shard_map/ppermute | solution.py:26
  19.6 1.4 copy-start.4
  21.0 0.7 copy-start.5
  21.7 55.1 %all-to-all-start.1 = ((bf16[16,64,896]{2,1,0:T(8,128)(2,1)}), bf16[16,64,896]{2,1,0:T(8,128)(2,1)S(1)}, u32[]{:S(2)}, u32[]{:S(2)}) async-start(bf16[16,64,896]{2,1,0:T(8,128)(2,1)} %encode_part.3), calls=%async_computation.1 | async-start | bytes 3670016 | tf_op jit(solution)/shard_map/all_to_all | solution.py:286
  76.8 1.3 copy-start.2
  78.1 47.3 %all-to-all-start = ((bf16[16,64,896]{2,1,0:T(8,128)(2,1)}), bf16[16,64,896]{2,1,0:T(8,128)(2,1)S(1)}, u32[]{:S(2)}, u32[]{:S(2)}) async-start(bf16[16,64,896]{2,1,0:T(8,128)(2,1)} %encode_part.2), calls=%async_computation | async-start | bytes 3670016 | tf_op jit(solution)/shard_map/all_to_all | solution.py:286
  82.1 2.7 %copy-start.6 = (s32[4]{0:T(128)S(1)}, s32[4]{0:T(128)}, u32[]{:S(2)}) copy-start(s32[4]{0:T(128)} %param.15) | copy-start | bytes 52
  82.1 2.8 %copy-start.7 = (s32[4,2]{0,1:T(2,128)S(1)}, s32[4,2]{0,1:T(2,128)}, u32[]{:S(2)}) copy-start(s32[4,2]{0,1:T(2,128)} %param.13) | copy-start | bytes 100
  125.3 1.2 copy-start.1
  146.5 13.0 %collective-permute-start.3 = (bf16[63,2048]{1,0:T(8,128)(2,1)S(1)}, bf16[63,2048]{1,0:T(8,128)(2,1)S(1)}, u32[]{:S(2)}, u32[]{:S(2)}) collective-permute-start(bf16[63,2048]{1,0:T(8,128)(2,1)S(1)} %slice.30), channel_id=1, source_target_pairs={{0,1},{1,2},{2,3},{3,4},{4,5},{5,6},{6,7},{7,8},{8,9},{9,10},{10,1... | collective-permute-start | bytes 774152 | tf_op jit(solution)/shard_map/ppermute | solution.py:26
  159.5 46.6 %all-to-all-start.2 = ((bf16[16,64,896]{2,1,0:T(8,128)(2,1)}), bf16[16,64,896]{2,1,0:T(8,128)(2,1)S(1)}, u32[]{:S(2)}, u32[]{:S(2)}) async-start(bf16[16,64,896]{2,1,0:T(8,128)(2,1)} %return_part.2), calls=%async_computation.2 | async-start | bytes 3670016 | tf_op jit(solution)/shard_map/all_to_all | solution.py:286
  172.9 37.7 %copy-start.3 = (bf16[256,2048]{1,0:T(8,128)(2,1)S(1)}, bf16[256,2048]{1,0:T(8,128)(2,1)}, u32[]{:S(2)}) copy-start(bf16[256,2048]{1,0:T(8,128)(2,1)} %get-tuple-element.25) | copy-start | bytes 3145732
  206.1 4.6 %copy-start = (bf16[16,64,896]{2,1,0:T(8,128)(2,1)}, bf16[16,64,896]{2,1,0:T(8,128)(2,1)S(1)}, u32[]{:S(2)}) copy-start(bf16[16,64,896]{2,1,0:T(8,128)(2,1)S(1)} %all-to-all-done.2.x_ref) | copy-start | bytes 5505028
  206.1 48.4 %all-to-all-start.3 = ((bf16[16,64,896]{2,1,0:T(8,128)(2,1)}), bf16[16,64,896]{2,1,0:T(8,128)(2,1)}, u32[]{:S(2)}, u32[]{:S(2)}) async-start(bf16[16,64,896]{2,1,0:T(8,128)(2,1)} %return_part.3), calls=%async_computation.3 | async-start | bytes 3670016 | tf_op jit(solution)/shard_map/all_to_all | solution.py:286

commit v3 on v2

--- a/solution.py
+++ b/solution.py
@@ -87,13 +87,15 @@
         held[n * rows : (n + 1) * rows] = x_ref[slot_ref[n]]
 
 
-def project_kernel(slots, slot_ref, x_ref, kw_ref, vw_ref, k_ref, v_ref, held):
+def project_kernel(slots, slot_ref, x_ref, kw_ref, vw_ref, k_ref, v_ref, kt_ref, vt_ref, held):
     @pl.when(pl.program_id(0) == 0)
     def _():
         gather_rows(slot_ref, x_ref, held, slots)
 
     k_ref[...] = dot(held[...], kw_ref[...]).astype(jnp.bfloat16)
     v_ref[...] = dot(held[...], vw_ref[...]).astype(jnp.bfloat16)
+    kt_ref[...] = kw_ref[...].T
+    vt_ref[...] = vw_ref[...].T
 
 
 def project_part(incoming, key_weight, value_weight, recv_slot):
@@ -104,6 +106,8 @@
     weight = pl.BlockSpec((width, wide), lambda j, s: (0, j))
     result = pl.BlockSpec((slots * rows, wide), lambda j, s: (0, j))
     shape = jax.ShapeDtypeStruct((slots * rows, features), jnp.bfloat16)
+    turned = pl.BlockSpec((wide, width), lambda j, s: (j, 0))
+    turned_shape = jax.ShapeDtypeStruct((features, width), jnp.bfloat16)
     return pl.pallas_call(
         functools.partial(project_kernel, slots),
         grid_spec=pltpu.PrefetchScalarGridSpec(
@@ -114,10 +118,10 @@
                 weight,
                 weight,
             ],
-            out_specs=[result, result],
+            out_specs=[result, result, turned, turned],
             scratch_shapes=[pltpu.VMEM((slots * rows, width), jnp.bfloat16)],
         ),
-        out_shape=[shape, shape],
+        out_shape=[shape, shape, turned_shape, turned_shape],
         cost_estimate=pl.CostEstimate(
             flops=4 * slots * rows * width * features,
             bytes_accessed=4 * width * features + 4 * slots * rows * features,
@@ -221,7 +225,7 @@
     def _():
         acc[...] = jnp.zeros_like(acc)
 
-    acc[...] += dot(gk_ref[...], kw_ref[...], NT) + dot(gv_ref[...], vw_ref[...], NT)
+    acc[...] += dot(gk_ref[...], kw_ref[...]) + dot(gv_ref[...], vw_ref[...])
 
     @pl.when(step == pl.num_programs(0) - 1)
     def _():
@@ -234,9 +238,9 @@
     slots = recv_slot.shape[0]
     total_rows, features = grad_keys.shape
     rows = total_rows // slots
-    width = key_weight.shape[0]
+    width = key_weight.shape[1]
     wide = features // 2
-    weight = pl.BlockSpec((width, wide), lambda j, s: (0, j))
+    weight = pl.BlockSpec((wide, width), lambda j, s: (j, 0))
     near = pl.BlockSpec((total_rows, wide), lambda j, s: (0, j))
     return pl.pallas_call(
         functools.partial(return_kernel, slots),
@@ -316,13 +320,16 @@
     recv_slot = owners * CAP + jnp.sum(same_owner.astype(jnp.int32), axis=1)
 
     label_send = (sequence_ids[:1] % 128 + 1).astype(jnp.bfloat16)
-    next_query, next_cot, next_label = from_behind(
-        (queries[:head_rows], cotangent[:head_rows], label_send), ("seq", "nbr"), -1
+    label_rows = jnp.broadcast_to(label_send[:, None], (2, features))
+    next_rows = from_behind(
+        jnp.concatenate([queries[:head_rows], cotangent[:head_rows], label_rows], 0),
+        ("seq", "nbr"),
+        -1,
     )
     sent_a = encode_part(0, neighbour_tokens, enc_in, enc_out, send_slot, slot_total)
-    sent_a, next_query, next_cot, next_label = lax.optimization_barrier(
-        (sent_a, next_query, next_cot, next_label)
-    )
+    sent_a, next_rows = lax.optimization_barrier((sent_a, next_rows))
+    next_query, next_cot = next_rows[:head_rows], next_rows[head_rows : 2 * head_rows]
+    next_label = next_rows[2 * head_rows, :1]
     in_a = exchange(sent_a)
     sent_b = encode_part(1, neighbour_tokens, enc_in, enc_out, send_slot, slot_total)
     in_b = exchange(sent_b)
@@ -335,15 +342,15 @@
     query_ext = jnp.concatenate([queries[head_rows:], next_query], 0)
     cot_ext = jnp.concatenate([cotangent[head_rows:], next_cot], 0)
 
-    keys_a, values_a = project_part(in_a, key_weight, value_weight, recv_slot)
+    keys_a, values_a, key_turned, value_turned = project_part(in_a, key_weight, value_weight, recv_slot)
     extended, gka, gva, gkb, gvb = attend_all(
         in_b, keys_a, values_a, key_weight, value_weight, query_ext, cot_ext, validity, recv_slot
     )
     carried = from_behind(extended[token_rows - head_rows :], ("seq", "nbr"), 1)
-    grads_a = return_part(gka, gva, key_weight, value_weight, recv_slot, slot_total)
+    grads_a = return_part(gka, gva, key_turned, value_turned, recv_slot, slot_total)
     grads_a, carried = lax.optimization_barrier((grads_a, carried))
     back_a = exchange(grads_a)
-    grads_b = return_part(gkb, gvb, key_weight, value_weight, recv_slot, slot_total)
+    grads_b = return_part(gkb, gvb, key_turned, value_turned, recv_slot, slot_total)
     back_a, grads_b = lax.optimization_barrier((back_a, grads_b))
     back_b = exchange(grads_b)
     attended = jnp.concatenate([carried, extended[: token_rows - head_rows]], 0)

time: 259 us -> 253 us (0.977)
  starting transfers between devices: 31.1 us -> 24 us
    all_to_all x4, starting transfers between devices: 23.8 us -> 19.3 us  [exchange(): return lax.all_to_all(block, 'nbr', split_axis=0, concat_axis=0, tiled=True)]
    ppermute x4 -> x2, waiting for transfers between devices: 1.42 us -> 5.69 us  [from_behind(): return lax.ppermute(block, axis, route)]
    all_to_all x4, waiting for transfers between devices: 133 us -> 129 us  [exchange(): return lax.all_to_all(block, 'nbr', split_axis=0, concat_axis=0, tiled=True)]
    ppermute x4 -> x2, starting transfers between devices: 7.27 us -> 4.69 us  [from_behind(): return lax.ppermute(block, axis, route)]
  transfers between devices with their start and end apart: 8 -> 6, of which waited for: 5 -> 5; matrix products, arithmetic and copies ran while one was open for 5% -> 4% of each run, Pallas kernels for 19% -> 20%
where the time goes in v3:
time: 253 us
  waiting for transfers between devices  135 us (53%)
  Pallas kernels  73.4 us (29%)
  starting transfers between devices  24 us (9%)
  local copies, waits for them, and re-layouts  12.5 us (5%)
  other arithmetic  5.25 us (2%)
  between operations  2.76 us (1%)
    all_to_all x4, waiting for transfers between devices, exchange(): return lax.all_to_all(block, 'nbr', split_axis=0, concat_axis=0, tiled=True)  129 us
    all_to_all x4, starting transfers between devices, exchange(): return lax.all_to_all(block, 'nbr', split_axis=0, concat_axis=0, tiled=True)  19.3 us
    pallas_call x2, Pallas kernels, return_part(): pl.pallas_call(functools.partial(return_kernel, slots), grid_spec=pltpu.P...  19.1 us
    pallas_call x1, Pallas kernels, attend_all(): pl.pallas_call(functools.partial(attend_kernel, slots, spans), grid_spec=...  19 us
    pallas_call x2, Pallas kernels, encode_part(): pl.pallas_call(encode_kernel, grid_spec=pltpu.PrefetchScalarGridSpec(num_...  18.1 us
    pallas_call x1, Pallas kernels, project_part(): pl.pallas_call(functools.partial(project_kernel, slots), grid_spec=pltpu....  10.9 us
    pallas_call x2, Pallas kernels, place(): pl.pallas_call(place_kernel, grid_spec=pltpu.PrefetchScalarGridSpec(num_s...  6.3 us
    ppermute x2, waiting for transfers between devices, from_behind(): return lax.ppermute(block, axis, route)  5.69 us
  transfers between devices with their start and end apart: 6, of which 5 were waited for; matrix products, arithmetic and copies ran while one was open for 4% of the time, Pallas kernels for 20%

profile of v3, /device:TPU:0, one launch (start us, length us, event | category | flops | bytes accessed | tf_op | source)
XLA Modules:
  0.0 252.5 jit_solution(17515429347146262419)
XLA Ops:
  0.6 0.0 copy-start.7
  2.6 1.0 slice.33
  3.6 1.0 slice.34
  4.6 0.1 pad.10.clone
  4.6 0.2 maximum_maximum_fusion
  4.8 1.3 collective-permute-start
  6.1 0.0 copy-done.7
  6.2 0.2 convert_reduce_fusion
  6.4 0.5 multiply_add_fusion.slot_ref
  6.9 9.1 %encode_part.3 = bf16[16,64,896]{2,1,0:T(8,128)(2,1)} custom-call(s32[8]{0:T(128)} %multiply_add_fusion.slot_ref, bf16[8,128,896]{2,1,0:T(8,128)(2,1)} %x_ref.3, bf16[896,1792]{1,0:T(8,128)(2,1)} %in_ref.3, bf16[1792,896]{1,0:T(8,128)(2,1)} %out_w_ref.3), custom_call_target="tpu_custom_call" | custom-call | flops 3288334336 | bytes 9175040 | tf_op jit(solution)/shard_map/encode_part/pallas_call | solution.py:58
  16.0 5.7 %collective-permute-done = bf16[128,2048]{1,0:T(8,128)(2,1)S(1)} collective-permute-done((bf16[128,2048]{1,0:T(8,128)(2,1)S(1)}, bf16[128,2048]{1,0:T(8,128)(2,1)S(1)}, u32[]{:S(2)}, u32[]{:S(2)}) %collective-permute-start) | collective-permute-done | bytes 524320 | tf_op jit(solution)/shard_map/ppermute | solution.py:26
  21.6 0.0 copy-start.4
  21.6 0.8 copy-done.4
  22.4 5.9 %all-to-all-start.1 = ((bf16[16,64,896]{2,1,0:T(8,128)(2,1)}), bf16[16,64,896]{2,1,0:T(8,128)(2,1)S(1)}, u32[]{:S(2)}, u32[]{:S(2)}) async-start(bf16[16,64,896]{2,1,0:T(8,128)(2,1)} %encode_part.3), calls=%async_computation.1 | async-start | bytes 3670016 | tf_op jit(solution)/shard_map/all_to_all | solution.py:290
  28.4 9.0 %encode_part.2 = bf16[16,64,896]{2,1,0:T(8,128)(2,1)} custom-call(s32[8]{0:T(128)} %multiply_add_fusion.slot_ref, bf16[8,128,896]{2,1,0:T(8,128)(2,1)} %x_ref.3, bf16[896,1792]{1,0:T(8,128)(2,1)} %in_ref.3, bf16[1792,896]{1,0:T(8,128)(2,1)} %out_w_ref.3), custom_call_target="tpu_custom_call" | custom-call | flops 3288334336 | bytes 9175040 | tf_op jit(solution)/shard_map/encode_part/pallas_call | solution.py:58
  37.4 33.3 %all-to-all-done.1.x_ref = bf16[16,64,896]{2,1,0:T(8,128)(2,1)S(1)} async-done(((bf16[16,64,896]{2,1,0:T(8,128)(2,1)}), bf16[16,64,896]{2,1,0:T(8,128)(2,1)S(1)}, u32[]{:S(2)}, u32[]{:S(2)}) %all-to-all-start.1) | async-done | bytes 1835040 | tf_op jit(solution)/shard_map/all_to_all | solution.py:290
  70.6 0.0 copy-start.2
  70.6 1.3 copy-done.2
  71.9 5.3 %all-to-all-start = ((bf16[16,64,896]{2,1,0:T(8,128)(2,1)}), bf16[16,64,896]{2,1,0:T(8,128)(2,1)S(1)}, u32[]{:S(2)}, u32[]{:S(2)}) async-start(bf16[16,64,896]{2,1,0:T(8,128)(2,1)} %encode_part.2), calls=%async_computation | async-start | bytes 3670016 | tf_op jit(solution)/shard_map/all_to_all | solution.py:290
  77.2 0.0 copy-start.5
  77.2 0.0 copy-start.6
  77.2 1.4 slice.36
  78.6 1.3 slice.38
  79.9 0.0 copy-done.5
  79.9 0.1 slice.40
  80.0 0.0 copy-done.6
  80.0 0.1 copy.16
  80.1 0.1 reshape.133
  80.2 0.2 convert_reduce_fusion.1
  80.4 0.6 multiply_add_fusion.1.slot_ref
  81.0 1.2 slice.41
  82.2 0.6 maximum_compare_fusion
  82.8 0.1 or_convert_fusion
  82.9 0.8 reshape.135.valid_ref
  83.7 1.1 fusion.6
  84.8 1.6 pad_maximum_fusion
  86.4 10.9 %project_part.1 = (bf16[512,2048]{1,0:T(8,128)(2,1)}, bf16[512,2048]{1,0:T(8,128)(2,1)}, bf16[2048,896]{1,0:T(8,128)(2,1)}, bf16[2048,896]{1,0:T(8,128)(2,1)}) custom-call(s32[8]{0:T(128)} %multiply_add_fusion.1.slot_ref, bf16[16,64,896]{2,1,0:T(8,128)(2,1)} %copy-done.2, bf16[896,2048]{1,0:T(8,128)(2,1)} %kw_ref.3, bf16[896,2048]{1,0:T(8,128)(2,1)} %vw_ref.3), custom_call_target="tpu_custom_call" | custom-call | flops 3758096384 | bytes 11534336 | tf_op jit(solution)/shard_map/project_part/pallas_call | solution.py:111
  97.2 23.5 %all-to-all-done.x_ref = bf16[16,64,896]{2,1,0:T(8,128)(2,1)S(1)} async-done(((bf16[16,64,896]{2,1,0:T(8,128)(2,1)}), bf16[16,64,896]{2,1,0:T(8,128)(2,1)S(1)}, u32[]{:S(2)}, u32[]{:S(2)}) %all-to-all-start) | async-done | bytes 1835040 | tf_op jit(solution)/shard_map/all_to_all | solution.py:290
  120.7 0.0 copy-start.1
  120.7 1.2 copy-done.1
  121.9 19.0 %attend_all.1 = (bf16[256,2048]{1,0:T(8,128)(2,1)}, bf16[512,2048]{1,0:T(8,128)(2,1)}, bf16[512,2048]{1,0:T(8,128)(2,1)}, bf16[512,2048]{1,0:T(8,128)(2,1)}, bf16[512,2048]{1,0:T(8,128)(2,1)}) custom-call(s32[8]{0:T(128)} %multiply_add_fusion.1.slot_ref, bf16[16,64,896]{2,1,0:T(8,128)(2,1)} %copy-done.1, bf16[512,2048]{1,0:T(8,128)(2,1)} %get-tuple-element.18.ka_ref, ...), custom_call_target="tpu_custom_call" | custom-call | flops 5100273664 | bytes 19922944 | tf_op jit(solution)/shard_map/attend_all/pallas_call | solution.py:193
  140.9 1.0 slice.42
  141.9 3.4 %collective-permute-start.1 = (bf16[63,2048]{1,0:T(8,128)(2,1)S(1)}, bf16[63,2048]{1,0:T(8,128)(2,1)S(1)}, u32[]{:S(2)}, u32[]{:S(2)}) collective-permute-start(bf16[63,2048]{1,0:T(8,128)(2,1)S(1)} %slice.42), channel_id=1, source_target_pairs={{0,1},{1,2},{2,3},{3,4},{4,5},{5,6},{6,7},{7,8},{8,9},{9,10},{10,1... | collective-permute-start | bytes 774152 | tf_op jit(solution)/shard_map/ppermute | solution.py:26
  145.3 9.5 %return_part.2 = bf16[16,64,896]{2,1,0:T(8,128)(2,1)} custom-call(s32[8]{0:T(128)} %multiply_add_fusion.1.slot_ref, bf16[512,2048]{1,0:T(8,128)(2,1)} %get-tuple-element.21.gk_ref, bf16[512,2048]{1,0:T(8,128)(2,1)} %get-tuple-element.22.gv_ref, bf16[2048,896]{1,0:T(8,128)(2,1)} %get-tuple-element.23.kw_ref, bf16[2048,896]{1,0:T(8,128)(2,1)} %get-tuple-element.24.vw_ref), custom_call_target="tpu_custom_call" | custom-call | flops 3758096384 | bytes 11534336 | tf_op jit(solution)/shard_map/return_part/pallas_call | solution.py:245
  154.9 0.0 collective-permute-done.1
  154.9 3.8 %all-to-all-start.2 = ((bf16[16,64,896]{2,1,0:T(8,128)(2,1)}), bf16[16,64,896]{2,1,0:T(8,128)(2,1)S(1)}, u32[]{:S(2)}, u32[]{:S(2)}) async-start(bf16[16,64,896]{2,1,0:T(8,128)(2,1)} %return_part.2), calls=%async_computation.2 | async-start | bytes 3670016 | tf_op jit(solution)/shard_map/all_to_all | solution.py:290
  158.6 9.6 %return_part.3 = bf16[16,64,896]{2,1,0:T(8,128)(2,1)} custom-call(s32[8]{0:T(128)} %multiply_add_fusion.1.slot_ref, bf16[512,2048]{1,0:T(8,128)(2,1)} %get-tuple-element.28.gk_ref, bf16[512,2048]{1,0:T(8,128)(2,1)} %get-tuple-element.29.gv_ref, bf16[2048,896]{1,0:T(8,128)(2,1)} %get-tuple-element.23.kw_ref, bf16[2048,896]{1,0:T(8,128)(2,1)} %get-tuple-element.24.vw_ref), custom_call_target="tpu_custom_call" | custom-call | flops 3758096384 | bytes 11534336 | tf_op jit(solution)/shard_map/return_part/pallas_call | solution.py:245
  168.3 0.0 copy-start.3
  168.3 34.0 %all-to-all-done.2.x_ref = bf16[16,64,896]{2,1,0:T(8,128)(2,1)S(1)} async-done(((bf16[16,64,896]{2,1,0:T(8,128)(2,1)}), bf16[16,64,896]{2,1,0:T(8,128)(2,1)S(1)}, u32[]{:S(2)}, u32[]{:S(2)}) %all-to-all-start.2) | async-done | bytes 1835040 | tf_op jit(solution)/shard_map/all_to_all | solution.py:290
  202.2 0.0 copy-start
  202.2 4.3 %all-to-all-start.3 = ((bf16[16,64,896]{2,1,0:T(8,128)(2,1)}), bf16[16,64,896]{2,1,0:T(8,128)(2,1)}, u32[]{:S(2)}, u32[]{:S(2)}) async-start(bf16[16,64,896]{2,1,0:T(8,128)(2,1)} %return_part.3), calls=%async_computation.3 | async-start | bytes 3670016 | tf_op jit(solution)/shard_map/all_to_all | solution.py:290
  206.6 0.0 copy-done.3
  206.6 0.1 slice.43
  206.6 0.0 copy-done
  206.6 1.2 pad_maximum_fusion.2
  207.9 3.1 %place.2.refs_0_ = bf16[8,128,896]{2,1,0:T(8,128)(2,1)} custom-call(s32[8]{0:T(128)} %multiply_add_fusion.slot_ref, bf16[16,64,896]{2,1,0:T(8,128)(2,1)} %copy-done), custom_call_target="tpu_custom_call" | custom-call | tf_op jit(solution)/shard_map/place/pallas_call | solution.py:274
  211.0 38.3 %all-to-all-done.3.x_ref = bf16[16,64,896]{2,1,0:T(8,128)(2,1)} async-done(((bf16[16,64,896]{2,1,0:T(8,128)(2,1)}), bf16[16,64,896]{2,1,0:T(8,128)(2,1)}, u32[]{:S(2)}, u32[]{:S(2)}) %all-to-all-start.3) | async-done | bytes 1835040 | tf_op jit(solution)/shard_map/all_to_all | solution.py:290
  249.4 3.2 %place.3 = bf16[8,128,896]{2,1,0:T(8,128)(2,1)} custom-call(s32[8]{0:T(128)} %multiply_add_fusion.slot_ref, bf16[16,64,896]{2,1,0:T(8,128)(2,1)} %all-to-all-done.3.x_ref, bf16[8,128,896]{2,1,0:T(8,128)(2,1)} %place.2.refs_0_), custom_call_target="tpu_custom_call", output_to_operand_aliasing={{}: (2, {})} | custom-call | tf_op jit(solution)/shard_map/place/pallas_call | solution.py:274
  (5 shorter events, 0.1 us)
Async XLA Ops:
  0.6 5.5 %copy-start.7 = (s32[8]{0:T(128)S(1)}, s32[8]{0:T(128)}, u32[]{:S(2)}) copy-start(s32[8]{0:T(128)} %param.14) | copy-start | bytes 100
  4.8 16.8 %collective-permute-start = (bf16[128,2048]{1,0:T(8,128)(2,1)S(1)}, bf16[128,2048]{1,0:T(8,128)(2,1)S(1)}, u32[]{:S(2)}, u32[]{:S(2)}) collective-permute-start(bf16[128,2048]{1,0:T(8,128)(2,1)S(1)} %maximum_maximum_fusion), channel_id=1, source_target_pairs={{1,0},{2,1},{3,2},{4,3},{5,4},{6,5},{7,6},{8,7},{9,8},{10,9},{11,1... | collective-permute-start | bytes 1572872 | tf_op jit(solution)/shard_map/ppermute | solution.py:26
  21.6 0.8 copy-start.4
  22.4 48.2 %all-to-all-start.1 = ((bf16[16,64,896]{2,1,0:T(8,128)(2,1)}), bf16[16,64,896]{2,1,0:T(8,128)(2,1)S(1)}, u32[]{:S(2)}, u32[]{:S(2)}) async-start(bf16[16,64,896]{2,1,0:T(8,128)(2,1)} %encode_part.3), calls=%async_computation.1 | async-start | bytes 3670016 | tf_op jit(solution)/shard_map/all_to_all | solution.py:290
  70.6 1.3 copy-start.2
  71.9 48.8 %all-to-all-start = ((bf16[16,64,896]{2,1,0:T(8,128)(2,1)}), bf16[16,64,896]{2,1,0:T(8,128)(2,1)S(1)}, u32[]{:S(2)}, u32[]{:S(2)}) async-start(bf16[16,64,896]{2,1,0:T(8,128)(2,1)} %encode_part.2), calls=%async_computation | async-start | bytes 3670016 | tf_op jit(solution)/shard_map/all_to_all | solution.py:290
  77.2 2.7 %copy-start.5 = (s32[4]{0:T(128)S(1)}, s32[4]{0:T(128)}, u32[]{:S(2)}) copy-start(s32[4]{0:T(128)} %param.15) | copy-start | bytes 52
  77.2 2.8 %copy-start.6 = (s32[4,2]{0,1:T(2,128)S(1)}, s32[4,2]{0,1:T(2,128)}, u32[]{:S(2)}) copy-start(s32[4,2]{0,1:T(2,128)} %param.13) | copy-start | bytes 100
  120.7 1.2 copy-start.1
  141.9 12.9 %collective-permute-start.1 = (bf16[63,2048]{1,0:T(8,128)(2,1)S(1)}, bf16[63,2048]{1,0:T(8,128)(2,1)S(1)}, u32[]{:S(2)}, u32[]{:S(2)}) collective-permute-start(bf16[63,2048]{1,0:T(8,128)(2,1)S(1)} %slice.42), channel_id=1, source_target_pairs={{0,1},{1,2},{2,3},{3,4},{4,5},{5,6},{6,7},{7,8},{8,9},{9,10},{10,1... | collective-permute-start | bytes 774152 | tf_op jit(solution)/shard_map/ppermute | solution.py:26
  154.9 47.4 %all-to-all-start.2 = ((bf16[16,64,896]{2,1,0:T(8,128)(2,1)}), bf16[16,64,896]{2,1,0:T(8,128)(2,1)S(1)}, u32[]{:S(2)}, u32[]{:S(2)}) async-start(bf16[16,64,896]{2,1,0:T(8,128)(2,1)} %return_part.2), calls=%async_computation.2 | async-start | bytes 3670016 | tf_op jit(solution)/shard_map/all_to_all | solution.py:290
  168.3 38.3 %copy-start.3 = (bf16[256,2048]{1,0:T(8,128)(2,1)S(1)}, bf16[256,2048]{1,0:T(8,128)(2,1)}, u32[]{:S(2)}) copy-start(bf16[256,2048]{1,0:T(8,128)(2,1)} %get-tuple-element.25) | copy-start | bytes 3145732
  202.2 4.4 %copy-start = (bf16[16,64,896]{2,1,0:T(8,128)(2,1)}, bf16[16,64,896]{2,1,0:T(8,128)(2,1)S(1)}, u32[]{:S(2)}) copy-start(bf16[16,64,896]{2,1,0:T(8,128)(2,1)S(1)} %all-to-all-done.2.x_ref) | copy-start | bytes 5505028
  202.2 47.1 %all-to-all-start.3 = ((bf16[16,64,896]{2,1,0:T(8,128)(2,1)}), bf16[16,64,896]{2,1,0:T(8,128)(2,1)}, u32[]{:S(2)}, u32[]{:S(2)}) async-start(bf16[16,64,896]{2,1,0:T(8,128)(2,1)} %return_part.3), calls=%async_computation.3 | async-start | bytes 3670016 | tf_op jit(solution)/shard_map/all_to_all | solution.py:290

commit v4 on v3

--- a/solution.py
+++ b/solution.py
@@ -133,11 +133,12 @@
 
 def attend_kernel(
     slots, spans, slot_ref, x_ref, ka_ref, va_ref, kw_ref, vw_ref, q_ref, c_ref, valid_ref,
-    out_ref, gka_ref, gva_ref, gkb_ref, gvb_ref, held,
+    out_ref, sent_ref, gkb_ref, gvb_ref, held, acc, gka_ref, gva_ref,
 ):
     @pl.when(pl.program_id(0) == 0)
     def _():
         gather_rows(slot_ref, x_ref, held, slots)
+        acc[...] = jnp.zeros_like(acc)
 
     inv_root = 1.0 / math.sqrt(HEAD_DIM)
     kb = dot(held[...], kw_ref[...]).astype(jnp.bfloat16)
@@ -177,6 +178,13 @@
         grad_keys = (dot(g, q_ref[m, f], TN) * inv_root).astype(jnp.bfloat16)
         gka_ref[n, f] = grad_keys[:half]
         gkb_ref[n, f] = grad_keys[half:]
+    acc[...] += dot(gka_ref[...], kw_ref[...], NT) + dot(gva_ref[...], vw_ref[...], NT)
+
+    @pl.when(pl.program_id(0) == pl.num_programs(0) - 1)
+    def _():
+        rows = sent_ref.shape[1]
+        for n in range(slots):
+            sent_ref[slot_ref[n]] = acc[n * rows : (n + 1) * rows].astype(jnp.bfloat16)
 
 
 def attend_all(incoming, keys_a, values_a, key_weight, value_weight, query, cot, valid, recv_slot):
@@ -205,12 +213,27 @@
                 mine,
                 pl.BlockSpec((tokens, 1), lambda j, s: (0, 0)),
             ],
-            out_specs=[mine, near, near, near, near],
-            scratch_shapes=[pltpu.VMEM((slots * rows, width), jnp.bfloat16)],
-        ),
-        out_shape=[jax.ShapeDtypeStruct((tokens, features), jnp.bfloat16)] + [shape] * 4,
+            out_specs=[
+                mine,
+                pl.BlockSpec((slot_total, rows, width), lambda j, s: (0, 0, 0)),
+                near,
+                near,
+            ],
+            scratch_shapes=[
+                pltpu.VMEM((slots * rows, width), jnp.bfloat16),
+                pltpu.VMEM((slots * rows, width), jnp.float32),
+                pltpu.VMEM((slots * rows, CHUNK), jnp.bfloat16),
+                pltpu.VMEM((slots * rows, CHUNK), jnp.bfloat16),
+            ],
+        ),
+        out_shape=[
+            jax.ShapeDtypeStruct((tokens, features), jnp.bfloat16),
+            jax.ShapeDtypeStruct((slot_total, rows, width), jnp.bfloat16),
+            shape,
+            shape,
+        ],
         cost_estimate=pl.CostEstimate(
-            flops=4 * slots * rows * width * features + 10 * tokens * positions * features,
+            flops=8 * slots * rows * width * features + 10 * tokens * positions * features,
             bytes_accessed=4 * width * features + 12 * slots * rows * features,
             transcendentals=tokens * positions * features // HEAD_DIM,
         ),
@@ -343,15 +366,14 @@
     cot_ext = jnp.concatenate([cotangent[head_rows:], next_cot], 0)
 
     keys_a, values_a, key_turned, value_turned = project_part(in_a, key_weight, value_weight, recv_slot)
-    extended, gka, gva, gkb, gvb = attend_all(
+    extended, grads_a, gkb, gvb = attend_all(
         in_b, keys_a, values_a, key_weight, value_weight, query_ext, cot_ext, validity, recv_slot
     )
-    carried = from_behind(extended[token_rows - head_rows :], ("seq", "nbr"), 1)
-    grads_a = return_part(gka, gva, key_turned, value_turned, recv_slot, slot_total)
-    grads_a, carried = lax.optimization_barrier((grads_a, carried))
     back_a = exchange(grads_a)
     grads_b = return_part(gkb, gvb, key_turned, value_turned, recv_slot, slot_total)
-    back_a, grads_b = lax.optimization_barrier((back_a, grads_b))
+    grads_b, extended = lax.optimization_barrier((grads_b, extended))
+    carried = from_behind(extended[token_rows - head_rows :], ("seq", "nbr"), 1)
+    back_a, grads_b, carried = lax.optimization_barrier((back_a, grads_b, carried))
     back_b = exchange(grads_b)
     attended = jnp.concatenate([carried, extended[: token_rows - head_rows]], 0)
     grad_encoded = place(1, back_b, send_slot, place(0, back_a, send_slot, None))

time: 253 us -> 249 us (0.984)
  waiting for transfers between devices: 135 us -> 129 us
  starting transfers between devices: 24 us -> 28.4 us
  Pallas kernels: 73.4 us -> 69.6 us
    all_to_all x4, waiting for transfers between devices: 129 us -> 116 us  [exchange(): return lax.all_to_all(block, 'nbr', split_axis=0, concat_axis=0, tiled=True)]
    pallas_call x2 -> x1, Pallas kernels: 19.1 us -> 9.62 us  [return_part(): pl.pallas_call(functools.partial(return_kernel, slots), grid_spec=pltpu.P...]
    ppermute x2, waiting for transfers between devices: 5.69 us -> 13 us  [from_behind(): return lax.ppermute(block, axis, route)]
    pallas_call x1, Pallas kernels: 19 us -> 24.8 us  [attend_all(): pl.pallas_call(functools.partial(attend_kernel, slots, spans), grid_spec=...]
    all_to_all x4, starting transfers between devices: 19.3 us -> 23.2 us  [exchange(): return lax.all_to_all(block, 'nbr', split_axis=0, concat_axis=0, tiled=True)]
  transfers between devices with their start and end apart: 6 -> 6, of which waited for: 5 -> 6; matrix products, arithmetic and copies ran while one was open for 4% -> 5% of each run, Pallas kernels for 20% -> 17%
where the time goes in v4:
time: 249 us; the launch traced here: 248 us
  waiting for transfers between devices  129 us (52%)
  Pallas kernels  69.6 us (28%)
  starting transfers between devices  28.4 us (11%)
  local copies, waits for them, and re-layouts  13.6 us (5%)
  other arithmetic  5.21 us (2%)
  between operations  2.73 us (1%)
    all_to_all x4, waiting for transfers between devices, exchange(): return lax.all_to_all(block, 'nbr', split_axis=0, concat_axis=0, tiled=True)  116 us
    pallas_call x1, Pallas kernels, attend_all(): pl.pallas_call(functools.partial(attend_kernel, slots, spans), grid_spec=...  24.8 us
    all_to_all x4, starting transfers between devices, exchange(): return lax.all_to_all(block, 'nbr', split_axis=0, concat_axis=0, tiled=True)  23.2 us
    pallas_call x2, Pallas kernels, encode_part(): pl.pallas_call(encode_kernel, grid_spec=pltpu.PrefetchScalarGridSpec(num_...  18.1 us
    ppermute x2, waiting for transfers between devices, from_behind(): return lax.ppermute(block, axis, route)  13 us
    pallas_call x1, Pallas kernels, project_part(): pl.pallas_call(functools.partial(project_kernel, slots), grid_spec=pltpu....  10.9 us
    pallas_call x1, Pallas kernels, return_part(): pl.pallas_call(functools.partial(return_kernel, slots), grid_spec=pltpu.P...  9.62 us
    pallas_call x2, Pallas kernels, place(): pl.pallas_call(place_kernel, grid_spec=pltpu.PrefetchScalarGridSpec(num_s...  6.3 us
  transfers between devices with their start and end apart: 6, of which 6 were waited for; matrix products, arithmetic and copies ran while one was open for 5% of the time, Pallas kernels for 17%

profile of v4, /device:TPU:0, one launch (start us, length us, event | category | flops | bytes accessed | tf_op | source)
XLA Modules:
  0.0 248.5 jit_solution(16699941656027391897)
XLA Ops:
  0.6 0.0 copy-start.6
  2.6 1.0 slice.33
  3.6 1.0 slice.34
  4.6 0.1 pad.10.clone
  4.6 0.2 maximum_maximum_fusion
  4.8 1.3 collective-permute-start
  6.1 0.0 copy-done.6
  6.2 0.2 convert_reduce_fusion
  6.4 0.5 multiply_add_fusion.slot_ref
  6.9 9.1 %encode_part.3 = bf16[16,64,896]{2,1,0:T(8,128)(2,1)} custom-call(s32[8]{0:T(128)} %multiply_add_fusion.slot_ref, bf16[8,128,896]{2,1,0:T(8,128)(2,1)} %x_ref.3, bf16[896,1792]{1,0:T(8,128)(2,1)} %in_ref.3, bf16[1792,896]{1,0:T(8,128)(2,1)} %out_w_ref.3), custom_call_target="tpu_custom_call" | custom-call | flops 3288334336 | bytes 9175040 | tf_op jit(solution)/shard_map/encode_part/pallas_call | solution.py:58
  15.9 5.7 %collective-permute-done = bf16[128,2048]{1,0:T(8,128)(2,1)S(1)} collective-permute-done((bf16[128,2048]{1,0:T(8,128)(2,1)S(1)}, bf16[128,2048]{1,0:T(8,128)(2,1)S(1)}, u32[]{:S(2)}, u32[]{:S(2)}) %collective-permute-start) | collective-permute-done | bytes 524320 | tf_op jit(solution)/shard_map/ppermute | solution.py:26
  21.6 0.0 copy-start.3
  21.6 0.8 copy-done.3
  22.4 5.9 %all-to-all-start.1 = ((bf16[16,64,896]{2,1,0:T(8,128)(2,1)}), bf16[16,64,896]{2,1,0:T(8,128)(2,1)S(1)}, u32[]{:S(2)}, u32[]{:S(2)}) async-start(bf16[16,64,896]{2,1,0:T(8,128)(2,1)} %encode_part.3), calls=%async_computation.1 | async-start | bytes 3670016 | tf_op jit(solution)/shard_map/all_to_all | solution.py:313
  28.4 9.0 %encode_part.2 = bf16[16,64,896]{2,1,0:T(8,128)(2,1)} custom-call(s32[8]{0:T(128)} %multiply_add_fusion.slot_ref, bf16[8,128,896]{2,1,0:T(8,128)(2,1)} %x_ref.3, bf16[896,1792]{1,0:T(8,128)(2,1)} %in_ref.3, bf16[1792,896]{1,0:T(8,128)(2,1)} %out_w_ref.3), custom_call_target="tpu_custom_call" | custom-call | flops 3288334336 | bytes 9175040 | tf_op jit(solution)/shard_map/encode_part/pallas_call | solution.py:58
  37.4 33.3 %all-to-all-done.1.x_ref = bf16[16,64,896]{2,1,0:T(8,128)(2,1)S(1)} async-done(((bf16[16,64,896]{2,1,0:T(8,128)(2,1)}), bf16[16,64,896]{2,1,0:T(8,128)(2,1)S(1)}, u32[]{:S(2)}, u32[]{:S(2)}) %all-to-all-start.1) | async-done | bytes 1835040 | tf_op jit(solution)/shard_map/all_to_all | solution.py:313
  70.6 0.0 copy-start.2
  70.6 1.3 copy-done.2
  71.9 5.3 %all-to-all-start = ((bf16[16,64,896]{2,1,0:T(8,128)(2,1)}), bf16[16,64,896]{2,1,0:T(8,128)(2,1)S(1)}, u32[]{:S(2)}, u32[]{:S(2)}) async-start(bf16[16,64,896]{2,1,0:T(8,128)(2,1)} %encode_part.2), calls=%async_computation | async-start | bytes 3670016 | tf_op jit(solution)/shard_map/all_to_all | solution.py:313
  77.2 0.0 copy-start.4
  77.2 0.0 copy-start.5
  77.2 1.4 slice.36
  78.6 1.3 slice.38
  79.9 0.0 copy-done.4
  79.9 0.1 slice.40
  80.0 0.0 copy-done.5
  80.0 0.1 copy.16
  80.1 0.1 reshape.133
  80.2 0.2 convert_reduce_fusion.1
  80.4 0.5 multiply_add_fusion.1.slot_ref
  80.9 1.2 slice.41
  82.1 0.7 maximum_compare_fusion
  82.9 0.1 or_convert_fusion
  82.9 0.8 reshape.135.valid_ref
  83.7 1.1 fusion.6
  84.8 1.6 pad_maximum_fusion
  86.4 10.9 %project_part.1 = (bf16[512,2048]{1,0:T(8,128)(2,1)}, bf16[512,2048]{1,0:T(8,128)(2,1)}, bf16[2048,896]{1,0:T(8,128)(2,1)}, bf16[2048,896]{1,0:T(8,128)(2,1)}) custom-call(s32[8]{0:T(128)} %multiply_add_fusion.1.slot_ref, bf16[16,64,896]{2,1,0:T(8,128)(2,1)} %copy-done.2, bf16[896,2048]{1,0:T(8,128)(2,1)} %kw_ref.3, bf16[896,2048]{1,0:T(8,128)(2,1)} %vw_ref.3), custom_call_target="tpu_custom_call" | custom-call | flops 3758096384 | bytes 11534336 | tf_op jit(solution)/shard_map/project_part/pallas_call | solution.py:111
  97.3 23.4 %all-to-all-done.x_ref = bf16[16,64,896]{2,1,0:T(8,128)(2,1)S(1)} async-done(((bf16[16,64,896]{2,1,0:T(8,128)(2,1)}), bf16[16,64,896]{2,1,0:T(8,128)(2,1)S(1)}, u32[]{:S(2)}, u32[]{:S(2)}) %all-to-all-start) | async-done | bytes 1835040 | tf_op jit(solution)/shard_map/all_to_all | solution.py:313
  120.7 0.0 copy-start.1
  120.7 1.2 copy-done.1
  121.9 24.8 %attend_all.1 = (bf16[256,2048]{1,0:T(8,128)(2,1)}, bf16[16,64,896]{2,1,0:T(8,128)(2,1)}, bf16[512,2048]{1,0:T(8,128)(2,1)}, bf16[512,2048]{1,0:T(8,128)(2,1)}) custom-call(s32[8]{0:T(128)} %multiply_add_fusion.1.slot_ref, bf16[16,64,896]{2,1,0:T(8,128)(2,1)} %copy-done.1, bf16[512,2048]{1,0:T(8,128)(2,1)} %get-tuple-element.18.ka_ref, ...), custom_call_target="tpu_custom_call" | custom-call | flops 8858370048 | bytes 19922944 | tf_op jit(solution)/shard_map/attend_all/pallas_call | solution.py:201
  146.7 3.6 %all-to-all-start.2 = ((bf16[16,64,896]{2,1,0:T(8,128)(2,1)}), bf16[16,64,896]{2,1,0:T(8,128)(2,1)S(1)}, u32[]{:S(2)}, u32[]{:S(2)}) async-start(bf16[16,64,896]{2,1,0:T(8,128)(2,1)} %get-tuple-element.21), calls=%async_computation.2 | async-start | bytes 3670016 | tf_op jit(solution)/shard_map/all_to_all | solution.py:313
  150.3 9.6 %return_part.1 = bf16[16,64,896]{2,1,0:T(8,128)(2,1)} custom-call(s32[8]{0:T(128)} %multiply_add_fusion.1.slot_ref, bf16[512,2048]{1,0:T(8,128)(2,1)} %get-tuple-element.22.gk_ref, bf16[512,2048]{1,0:T(8,128)(2,1)} %get-tuple-element.23.gv_ref, bf16[2048,896]{1,0:T(8,128)(2,1)} %get-tuple-element.24.kw_ref, bf16[2048,896]{1,0:T(8,128)(2,1)} %get-tuple-element.25.vw_ref), custom_call_target="tpu_custom_call" | custom-call | flops 3758096384 | bytes 11534336 | tf_op jit(solution)/shard_map/return_part/pallas_call | solution.py:268
  159.9 1.0 slice.42
  161.0 3.9 %collective-permute-start.1 = (bf16[63,2048]{1,0:T(8,128)(2,1)S(1)}, bf16[63,2048]{1,0:T(8,128)(2,1)S(1)}, u32[]{:S(2)}, u32[]{:S(2)}) collective-permute-start(bf16[63,2048]{1,0:T(8,128)(2,1)S(1)} %slice.42), channel_id=1, source_target_pairs={{0,1},{1,2},{2,3},{3,4},{4,5},{5,6},{6,7},{7,8},{8,9},{9,10},{10,1... | collective-permute-start | bytes 774152 | tf_op jit(solution)/shard_map/ppermute | solution.py:26
  164.9 7.3 %collective-permute-done.1 = bf16[63,2048]{1,0:T(8,128)(2,1)S(1)} collective-permute-done((bf16[63,2048]{1,0:T(8,128)(2,1)S(1)}, bf16[63,2048]{1,0:T(8,128)(2,1)S(1)}, u32[]{:S(2)}, u32[]{:S(2)}) %collective-permute-start.1) | collective-permute-done | bytes 258080 | tf_op jit(solution)/shard_map/ppermute | solution.py:26
  172.2 21.0 %all-to-all-done.2.x_ref = bf16[16,64,896]{2,1,0:T(8,128)(2,1)S(1)} async-done(((bf16[16,64,896]{2,1,0:T(8,128)(2,1)}), bf16[16,64,896]{2,1,0:T(8,128)(2,1)S(1)}, u32[]{:S(2)}, u32[]{:S(2)}) %all-to-all-start.2) | async-done | bytes 1835040 | tf_op jit(solution)/shard_map/all_to_all | solution.py:313
  193.2 0.0 copy-start
  193.2 8.4 %all-to-all-start.3 = ((bf16[16,64,896]{2,1,0:T(8,128)(2,1)}), bf16[16,64,896]{2,1,0:T(8,128)(2,1)}, u32[]{:S(2)}, u32[]{:S(2)}) async-start(bf16[16,64,896]{2,1,0:T(8,128)(2,1)} %return_part.1), calls=%async_computation.3 | async-start | bytes 3670016 | tf_op jit(solution)/shard_map/all_to_all | solution.py:313
  201.6 1.2 slice.43
  202.8 0.0 copy-done
  202.8 3.2 %place.2.refs_0_ = bf16[8,128,896]{2,1,0:T(8,128)(2,1)} custom-call(s32[8]{0:T(128)} %multiply_add_fusion.slot_ref, bf16[16,64,896]{2,1,0:T(8,128)(2,1)} %copy-done), custom_call_target="tpu_custom_call" | custom-call | tf_op jit(solution)/shard_map/place/pallas_call | solution.py:297
  205.9 1.2 pad_maximum_fusion.2
  207.1 38.2 %all-to-all-done.3.x_ref = bf16[16,64,896]{2,1,0:T(8,128)(2,1)} async-done(((bf16[16,64,896]{2,1,0:T(8,128)(2,1)}), bf16[16,64,896]{2,1,0:T(8,128)(2,1)}, u32[]{:S(2)}, u32[]{:S(2)}) %all-to-all-start.3) | async-done | bytes 1835040 | tf_op jit(solution)/shard_map/all_to_all | solution.py:313
  245.3 3.2 %place.3 = bf16[8,128,896]{2,1,0:T(8,128)(2,1)} custom-call(s32[8]{0:T(128)} %multiply_add_fusion.slot_ref, bf16[16,64,896]{2,1,0:T(8,128)(2,1)} %all-to-all-done.3.x_ref, bf16[8,128,896]{2,1,0:T(8,128)(2,1)} %place.2.refs_0_), custom_call_target="tpu_custom_call", output_to_operand_aliasing={{}: (2, {})} | custom-call | tf_op jit(solution)/shard_map/place/pallas_call | solution.py:297
  (5 shorter events, 0.1 us)
Async XLA Ops:
  0.6 5.5 %copy-start.6 = (s32[8]{0:T(128)S(1)}, s32[8]{0:T(128)}, u32[]{:S(2)}) copy-start(s32[8]{0:T(128)} %param.14) | copy-start | bytes 100
  4.8 16.8 %collective-permute-start = (bf16[128,2048]{1,0:T(8,128)(2,1)S(1)}, bf16[128,2048]{1,0:T(8,128)(2,1)S(1)}, u32[]{:S(2)}, u32[]{:S(2)}) collective-permute-start(bf16[128,2048]{1,0:T(8,128)(2,1)S(1)} %maximum_maximum_fusion), channel_id=1, source_target_pairs={{1,0},{2,1},{3,2},{4,3},{5,4},{6,5},{7,6},{8,7},{9,8},{10,9},{11,1... | collective-permute-start | bytes 1572872 | tf_op jit(solution)/shard_map/ppermute | solution.py:26
  21.6 0.8 copy-start.3
  22.4 48.2 %all-to-all-start.1 = ((bf16[16,64,896]{2,1,0:T(8,128)(2,1)}), bf16[16,64,896]{2,1,0:T(8,128)(2,1)S(1)}, u32[]{:S(2)}, u32[]{:S(2)}) async-start(bf16[16,64,896]{2,1,0:T(8,128)(2,1)} %encode_part.3), calls=%async_computation.1 | async-start | bytes 3670016 | tf_op jit(solution)/shard_map/all_to_all | solution.py:313
  70.6 1.3 copy-start.2
  71.9 48.8 %all-to-all-start = ((bf16[16,64,896]{2,1,0:T(8,128)(2,1)}), bf16[16,64,896]{2,1,0:T(8,128)(2,1)S(1)}, u32[]{:S(2)}, u32[]{:S(2)}) async-start(bf16[16,64,896]{2,1,0:T(8,128)(2,1)} %encode_part.2), calls=%async_computation | async-start | bytes 3670016 | tf_op jit(solution)/shard_map/all_to_all | solution.py:313
  77.2 2.7 %copy-start.4 = (s32[4]{0:T(128)S(1)}, s32[4]{0:T(128)}, u32[]{:S(2)}) copy-start(s32[4]{0:T(128)} %param.15) | copy-start | bytes 52
  77.2 2.8 %copy-start.5 = (s32[4,2]{0,1:T(2,128)S(1)}, s32[4,2]{0,1:T(2,128)}, u32[]{:S(2)}) copy-start(s32[4,2]{0,1:T(2,128)} %param.13) | copy-start | bytes 100
  120.7 1.2 copy-start.1
  146.7 46.5 %all-to-all-start.2 = ((bf16[16,64,896]{2,1,0:T(8,128)(2,1)}), bf16[16,64,896]{2,1,0:T(8,128)(2,1)S(1)}, u32[]{:S(2)}, u32[]{:S(2)}) async-start(bf16[16,64,896]{2,1,0:T(8,128)(2,1)} %get-tuple-element.21), calls=%async_computation.2 | async-start | bytes 3670016 | tf_op jit(solution)/shard_map/all_to_all | solution.py:313
  161.0 11.2 %collective-permute-start.1 = (bf16[63,2048]{1,0:T(8,128)(2,1)S(1)}, bf16[63,2048]{1,0:T(8,128)(2,1)S(1)}, u32[]{:S(2)}, u32[]{:S(2)}) collective-permute-start(bf16[63,2048]{1,0:T(8,128)(2,1)S(1)} %slice.42), channel_id=1, source_target_pairs={{0,1},{1,2},{2,3},{3,4},{4,5},{5,6},{6,7},{7,8},{8,9},{9,10},{10,1... | collective-permute-start | bytes 774152 | tf_op jit(solution)/shard_map/ppermute | solution.py:26
  193.2 9.6 %copy-start = (bf16[16,64,896]{2,1,0:T(8,128)(2,1)}, bf16[16,64,896]{2,1,0:T(8,128)(2,1)S(1)}, u32[]{:S(2)}) copy-start(bf16[16,64,896]{2,1,0:T(8,128)(2,1)S(1)} %all-to-all-done.2.x_ref) | copy-start | bytes 5505028
  193.2 52.1 %all-to-all-start.3 = ((bf16[16,64,896]{2,1,0:T(8,128)(2,1)}), bf16[16,64,896]{2,1,0:T(8,128)(2,1)}, u32[]{:S(2)}, u32[]{:S(2)}) async-start(bf16[16,64,896]{2,1,0:T(8,128)(2,1)} %return_part.1), calls=%async_computation.3 | async-start | bytes 3670016 | tf_op jit(solution)/shard_map/all_to_all | solution.py:313

commit v5 on v4

--- a/solution.py
+++ b/solution.py
@@ -87,15 +87,13 @@
         held[n * rows : (n + 1) * rows] = x_ref[slot_ref[n]]
 
 
-def project_kernel(slots, slot_ref, x_ref, kw_ref, vw_ref, k_ref, v_ref, kt_ref, vt_ref, held):
+def project_kernel(slots, slot_ref, x_ref, kw_ref, vw_ref, k_ref, v_ref, held):
     @pl.when(pl.program_id(0) == 0)
     def _():
         gather_rows(slot_ref, x_ref, held, slots)
 
     k_ref[...] = dot(held[...], kw_ref[...]).astype(jnp.bfloat16)
     v_ref[...] = dot(held[...], vw_ref[...]).astype(jnp.bfloat16)
-    kt_ref[...] = kw_ref[...].T
-    vt_ref[...] = vw_ref[...].T
 
 
 def project_part(incoming, key_weight, value_weight, recv_slot):
@@ -106,8 +104,6 @@
     weight = pl.BlockSpec((width, wide), lambda j, s: (0, j))
     result = pl.BlockSpec((slots * rows, wide), lambda j, s: (0, j))
     shape = jax.ShapeDtypeStruct((slots * rows, features), jnp.bfloat16)
-    turned = pl.BlockSpec((wide, width), lambda j, s: (j, 0))
-    turned_shape = jax.ShapeDtypeStruct((features, width), jnp.bfloat16)
     return pl.pallas_call(
         functools.partial(project_kernel, slots),
         grid_spec=pltpu.PrefetchScalarGridSpec(
@@ -118,10 +114,10 @@
                 weight,
                 weight,
             ],
-            out_specs=[result, result, turned, turned],
+            out_specs=[result, result],
             scratch_shapes=[pltpu.VMEM((slots * rows, width), jnp.bfloat16)],
         ),
-        out_shape=[shape, shape, turned_shape, turned_shape],
+        out_shape=[shape, shape],
         cost_estimate=pl.CostEstimate(
             flops=4 * slots * rows * width * features,
             bytes_accessed=4 * width * features + 4 * slots * rows * features,
@@ -133,7 +129,7 @@
 
 def attend_kernel(
     slots, spans, slot_ref, x_ref, ka_ref, va_ref, kw_ref, vw_ref, q_ref, c_ref, valid_ref,
-    out_ref, sent_ref, gkb_ref, gvb_ref, held, acc, gka_ref, gva_ref,
+    out_ref, sent_ref, held, acc, gk_ref, gv_ref,
 ):
     @pl.when(pl.program_id(0) == 0)
     def _():
@@ -172,19 +168,26 @@
         out_ref[m, f] = (dot(w, v) * valid_ref[m]).astype(jnp.bfloat16)
     for (n, _, f), w, g in zip(units, weights, masked):
         grad_values = dot(w, g, TN).astype(jnp.bfloat16)
-        gva_ref[n, f] = grad_values[:half]
-        gvb_ref[n, f] = grad_values[half:]
+        gv_ref[0, n, f] = grad_values[:half]
+        gv_ref[1, n, f] = grad_values[half:]
     for (n, m, f), g in zip(units, grad_scores):
         grad_keys = (dot(g, q_ref[m, f], TN) * inv_root).astype(jnp.bfloat16)
-        gka_ref[n, f] = grad_keys[:half]
-        gkb_ref[n, f] = grad_keys[half:]
-    acc[...] += dot(gka_ref[...], kw_ref[...], NT) + dot(gva_ref[...], vw_ref[...], NT)
+        gk_ref[0, n, f] = grad_keys[:half]
+        gk_ref[1, n, f] = grad_keys[half:]
+    total, wide = acc.shape[0], gk_ref.shape[2]
+    grad_keys = gk_ref[...].reshape(total, wide)
+    grad_values = gv_ref[...].reshape(total, wide)
+    acc[...] += dot(grad_keys, kw_ref[...], NT) + dot(grad_values, vw_ref[...], NT)
 
     @pl.when(pl.program_id(0) == pl.num_programs(0) - 1)
     def _():
-        rows = sent_ref.shape[1]
-        for n in range(slots):
-            sent_ref[slot_ref[n]] = acc[n * rows : (n + 1) * rows].astype(jnp.bfloat16)
+        rows = sent_ref.shape[1] // PARTS
+        for part in range(PARTS):
+            for n in range(slots):
+                at = (part * slots + n) * rows
+                sent_ref[slot_ref[n], part * rows : (part + 1) * rows] = acc[
+                    at : at + rows
+                ].astype(jnp.bfloat16)
 
 
 def attend_all(incoming, keys_a, values_a, key_weight, value_weight, query, cot, valid, recv_slot):
@@ -196,7 +199,6 @@
     weight = pl.BlockSpec((width, CHUNK), lambda j, s: (0, j))
     near = pl.BlockSpec((slots * rows, CHUNK), lambda j, s: (0, j))
     mine = pl.BlockSpec((tokens, CHUNK), lambda j, s: (0, j))
-    shape = jax.ShapeDtypeStruct((slots * rows, features), jnp.bfloat16)
     positions = PARTS * slots * rows // spans
     return pl.pallas_call(
         functools.partial(attend_kernel, slots, spans),
@@ -215,25 +217,21 @@
             ],
             out_specs=[
                 mine,
-                pl.BlockSpec((slot_total, rows, width), lambda j, s: (0, 0, 0)),
-                near,
-                near,
+                pl.BlockSpec((slot_total, PARTS * rows, width), lambda j, s: (0, 0, 0)),
             ],
             scratch_shapes=[
                 pltpu.VMEM((slots * rows, width), jnp.bfloat16),
-                pltpu.VMEM((slots * rows, width), jnp.float32),
-                pltpu.VMEM((slots * rows, CHUNK), jnp.bfloat16),
-                pltpu.VMEM((slots * rows, CHUNK), jnp.bfloat16),
+                pltpu.VMEM((PARTS * slots * rows, width), jnp.float32),
+                pltpu.VMEM((PARTS, slots * rows, CHUNK), jnp.bfloat16),
+                pltpu.VMEM((PARTS, slots * rows, CHUNK), jnp.bfloat16),
             ],
         ),
         out_shape=[
             jax.ShapeDtypeStruct((tokens, features), jnp.bfloat16),
-            jax.ShapeDtypeStruct((slot_total, rows, width), jnp.bfloat16),
-            shape,
-            shape,
+            jax.ShapeDtypeStruct((slot_total, PARTS * rows, width), jnp.bfloat16),
         ],
         cost_estimate=pl.CostEstimate(
-            flops=8 * slots * rows * width * features + 10 * tokens * positions * features,
+            flops=12 * slots * rows * width * features + 10 * tokens * positions * features,
             bytes_accessed=4 * width * features + 12 * slots * rows * features,
             transcendentals=tokens * positions * features // HEAD_DIM,
         ),
@@ -241,72 +239,26 @@
     )(recv_slot, incoming, keys_a, values_a, key_weight, value_weight, query, cot, column)
 
 
-def return_kernel(slots, slot_ref, gk_ref, gv_ref, kw_ref, vw_ref, out_ref, acc):
-    step = pl.program_id(0)
-
-    @pl.when(step == 0)
-    def _():
-        acc[...] = jnp.zeros_like(acc)
-
-    acc[...] += dot(gk_ref[...], kw_ref[...]) + dot(gv_ref[...], vw_ref[...])
-
-    @pl.when(step == pl.num_programs(0) - 1)
-    def _():
-        rows = out_ref.shape[1]
-        for n in range(slots):
-            out_ref[slot_ref[n]] = acc[n * rows : (n + 1) * rows].astype(jnp.bfloat16)
-
-
-def return_part(grad_keys, grad_values, key_weight, value_weight, recv_slot, slot_total):
-    slots = recv_slot.shape[0]
-    total_rows, features = grad_keys.shape
-    rows = total_rows // slots
-    width = key_weight.shape[1]
-    wide = features // 2
-    weight = pl.BlockSpec((wide, width), lambda j, s: (j, 0))
-    near = pl.BlockSpec((total_rows, wide), lambda j, s: (0, j))
-    return pl.pallas_call(
-        functools.partial(return_kernel, slots),
-        grid_spec=pltpu.PrefetchScalarGridSpec(
-            num_scalar_prefetch=1,
-            grid=(features // wide,),
-            in_specs=[near, near, weight, weight],
-            out_specs=pl.BlockSpec((slot_total, rows, width), lambda j, s: (0, 0, 0)),
-            scratch_shapes=[pltpu.VMEM((total_rows, width), jnp.float32)],
-        ),
-        out_shape=jax.ShapeDtypeStruct((slot_total, rows, width), jnp.bfloat16),
-        cost_estimate=pl.CostEstimate(
-            flops=4 * total_rows * width * features,
-            bytes_accessed=4 * width * features + 4 * total_rows * features,
-            transcendentals=0,
-        ),
-        name="return_part",
-    )(recv_slot, grad_keys, grad_values, key_weight, value_weight)
-
-
-def place_kernel(slot_ref, x_ref, *refs):
-    out_ref = refs[-1]
+def place_kernel(slot_ref, x_ref, out_ref):
     for n in range(out_ref.shape[0]):
         out_ref[n] = x_ref[slot_ref[n]]
 
 
-def place(part, returned, send_slot, partial):
+def place(returned, send_slot):
     slot_total, rows, width = returned.shape
     count = send_slot.shape[0]
-    whole = [] if partial is None else [partial]
+    strip = rows // 4
     return pl.pallas_call(
         place_kernel,
         grid_spec=pltpu.PrefetchScalarGridSpec(
             num_scalar_prefetch=1,
-            grid=(1,),
-            in_specs=[pl.BlockSpec((slot_total, rows, width), lambda n, s: (0, 0, 0))]
-            + [pl.BlockSpec(memory_space=pl.ANY)] * len(whole),
-            out_specs=pl.BlockSpec((count, rows, width), lambda n, s: (0, part, 0)),
-        ),
-        out_shape=jax.ShapeDtypeStruct((count, PARTS * rows, width), jnp.bfloat16),
-        input_output_aliases={2: 0} if whole else {},
+            grid=(rows // strip,),
+            in_specs=[pl.BlockSpec((slot_total, strip, width), lambda n, s: (0, n, 0))],
+            out_specs=pl.BlockSpec((count, strip, width), lambda n, s: (0, n, 0)),
+        ),
+        out_shape=jax.ShapeDtypeStruct((count, rows, width), jnp.bfloat16),
         name="place",
-    )(send_slot, returned, *whole)
+    )(send_slot, returned)
 
 
 def exchange(block):
@@ -365,18 +317,14 @@
     query_ext = jnp.concatenate([queries[head_rows:], next_query], 0)
     cot_ext = jnp.concatenate([cotangent[head_rows:], next_cot], 0)
 
-    keys_a, values_a, key_turned, value_turned = project_part(in_a, key_weight, value_weight, recv_slot)
-    extended, grads_a, gkb, gvb = attend_all(
+    keys_a, values_a = project_part(in_a, key_weight, value_weight, recv_slot)
+    extended, slot_grads = attend_all(
         in_b, keys_a, values_a, key_weight, value_weight, query_ext, cot_ext, validity, recv_slot
     )
-    back_a = exchange(grads_a)
-    grads_b = return_part(gkb, gvb, key_turned, value_turned, recv_slot, slot_total)
-    grads_b, extended = lax.optimization_barrier((grads_b, extended))
+    returned = exchange(slot_grads)
     carried = from_behind(extended[token_rows - head_rows :], ("seq", "nbr"), 1)
-    back_a, grads_b, carried = lax.optimization_barrier((back_a, grads_b, carried))
-    back_b = exchange(grads_b)
     attended = jnp.concatenate([carried, extended[: token_rows - head_rows]], 0)
-    grad_encoded = place(1, back_b, send_slot, place(0, back_a, send_slot, None))
+    grad_encoded = place(returned, send_slot)
     return (attended, grad_encoded)
 
 

time: 249 us -> 246 us (0.988)
  the two profiles are of different devices: /device:TPU:0 before, /device:TPU:17 now
where the time goes in v5:
time: 246 us; the launch traced here: 245 us
  waiting for transfers between devices  136 us (55%)
  Pallas kernels  61.8 us (25%)
  starting transfers between devices  31 us (13%)
  local copies, waits for them, and re-layouts  8.26 us (3%)
  other arithmetic  5.28 us (2%)
  between operations  2.73 us (1%)
    ppermute x2, waiting for transfers between devices, from_behind(): return lax.ppermute(block, axis, route)  85.5 us
    all_to_all x3, waiting for transfers between devices, exchange(): return lax.all_to_all(block, 'nbr', split_axis=0, concat_axis=0, tiled=True)  50.6 us
    pallas_call x1, Pallas kernels, attend_all(): pl.pallas_call(functools.partial(attend_kernel, slots, spans), grid_spec=...  29.5 us
    all_to_all x3, starting transfers between devices, exchange(): return lax.all_to_all(block, 'nbr', split_axis=0, concat_axis=0, tiled=True)  24.9 us
    pallas_call x2, Pallas kernels, encode_part(): pl.pallas_call(encode_kernel, grid_spec=pltpu.PrefetchScalarGridSpec(num_...  18.1 us
    pallas_call x1, Pallas kernels, project_part(): pl.pallas_call(functools.partial(project_kernel, slots), grid_spec=pltpu....  9.54 us
    ppermute x2, starting transfers between devices, from_behind(): return lax.ppermute(block, axis, route)  6.1 us
  transfers between devices with their start and end apart: 5, of which 4 were waited for; matrix products, arithmetic and copies ran while one was open for 5% of the time, Pallas kernels for 11%

profile of v5, /device:TPU:17, one launch (start us, length us, event | category | flops | bytes accessed | tf_op | source)
XLA Modules:
  0.0 245.2 jit_solution(8609924247217855149)
XLA Ops:
  0.6 0.0 copy-start.5
  2.6 1.0 slice.33
  3.6 1.0 slice.34
  4.6 0.1 pad.10.clone
  4.6 0.2 maximum_maximum_fusion
  4.8 3.0 %collective-permute-start = (bf16[128,2048]{1,0:T(8,128)(2,1)S(1)}, bf16[128,2048]{1,0:T(8,128)(2,1)S(1)}, u32[]{:S(2)}, u32[]{:S(2)}) collective-permute-start(bf16[128,2048]{1,0:T(8,128)(2,1)S(1)} %maximum_maximum_fusion), channel_id=1, source_target_pairs={{1,0},{2,1},{3,2},{4,3},{5,4},{6,5},{7,6},{8,7},{9,8},{10,9},{11,1... | collective-permute-start | bytes 1572872 | tf_op jit(solution)/shard_map/ppermute | solution.py:26
  7.9 0.0 copy-done.5
  7.9 0.2 convert_reduce_fusion
  8.1 0.5 multiply_add_fusion.slot_ref
  8.6 9.1 %encode_part.3 = bf16[16,64,896]{2,1,0:T(8,128)(2,1)} custom-call(s32[8]{0:T(128)} %multiply_add_fusion.slot_ref, bf16[8,128,896]{2,1,0:T(8,128)(2,1)} %x_ref.3, bf16[896,1792]{1,0:T(8,128)(2,1)} %in_ref.3, bf16[1792,896]{1,0:T(8,128)(2,1)} %out_w_ref.3), custom_call_target="tpu_custom_call" | custom-call | flops 3288334336 | bytes 9175040 | tf_op jit(solution)/shard_map/encode_part/pallas_call | solution.py:58
  17.7 1.9 collective-permute-done
  19.6 0.0 copy-start.2
  19.6 10.5 %all-to-all-start.1 = ((bf16[16,64,896]{2,1,0:T(8,128)(2,1)}), bf16[16,64,896]{2,1,0:T(8,128)(2,1)S(1)}, u32[]{:S(2)}, u32[]{:S(2)}) async-start(bf16[16,64,896]{2,1,0:T(8,128)(2,1)} %encode_part.3), calls=%async_computation.1 | async-start | bytes 3670016 | tf_op jit(solution)/shard_map/all_to_all | solution.py:265
  30.1 9.0 %encode_part.2 = bf16[16,64,896]{2,1,0:T(8,128)(2,1)} custom-call(s32[8]{0:T(128)} %multiply_add_fusion.slot_ref, bf16[8,128,896]{2,1,0:T(8,128)(2,1)} %x_ref.3, bf16[896,1792]{1,0:T(8,128)(2,1)} %in_ref.3, bf16[1792,896]{1,0:T(8,128)(2,1)} %out_w_ref.3), custom_call_target="tpu_custom_call" | custom-call | flops 3288334336 | bytes 9175040 | tf_op jit(solution)/shard_map/encode_part/pallas_call | solution.py:58
  39.1 0.0 copy-done.2
  39.1 29.0 %all-to-all-done.1.x_ref = bf16[16,64,896]{2,1,0:T(8,128)(2,1)S(1)} async-done(((bf16[16,64,896]{2,1,0:T(8,128)(2,1)}), bf16[16,64,896]{2,1,0:T(8,128)(2,1)S(1)}, u32[]{:S(2)}, u32[]{:S(2)}) %all-to-all-start.1) | async-done | bytes 1835040 | tf_op jit(solution)/shard_map/all_to_all | solution.py:265
  68.1 0.0 copy-start
  68.1 6.9 %all-to-all-start = ((bf16[16,64,896]{2,1,0:T(8,128)(2,1)}), bf16[16,64,896]{2,1,0:T(8,128)(2,1)}, u32[]{:S(2)}, u32[]{:S(2)}) async-start(bf16[16,64,896]{2,1,0:T(8,128)(2,1)} %encode_part.2), calls=%async_computation | async-start | bytes 3670016 | tf_op jit(solution)/shard_map/all_to_all | solution.py:265
  75.0 0.0 copy-start.3
  75.0 0.0 copy-start.4
  75.0 1.4 slice.36
  76.4 0.0 copy-done
  76.4 1.3 slice.38
  77.7 0.0 copy-done.3
  77.8 0.1 slice.40
  77.8 0.0 copy-done.4
  77.8 0.1 copy.15
  77.9 0.1 reshape.133
  78.0 0.2 convert_reduce_fusion.1
  78.2 0.5 multiply_add_fusion.1.slot_ref
  78.8 1.3 slice.41
  80.0 0.7 maximum_compare_fusion
  80.7 0.1 or_convert_fusion
  80.8 0.8 reshape.135.valid_ref
  81.6 1.1 fusion.6
  82.7 1.6 pad_maximum_fusion
  84.3 9.5 %project_part.1 = (bf16[512,2048]{1,0:T(8,128)(2,1)}, bf16[512,2048]{1,0:T(8,128)(2,1)}) custom-call(s32[8]{0:T(128)} %multiply_add_fusion.1.slot_ref, bf16[16,64,896]{2,1,0:T(8,128)(2,1)} %copy-done, bf16[896,2048]{1,0:T(8,128)(2,1)} %kw_ref.3, bf16[896,2048]{1,0:T(8,128)(2,1)} %vw_ref.3), custom_call_target="tpu_custom_call" | custom-call | flops 3758096384 | bytes 11534336 | tf_op jit(solution)/shard_map/project_part/pallas_call | solution.py:107
  93.8 21.6 %all-to-all-done.x_ref = bf16[16,64,896]{2,1,0:T(8,128)(2,1)} async-done(((bf16[16,64,896]{2,1,0:T(8,128)(2,1)}), bf16[16,64,896]{2,1,0:T(8,128)(2,1)}, u32[]{:S(2)}, u32[]{:S(2)}) %all-to-all-start) | async-done | bytes 1835040 | tf_op jit(solution)/shard_map/all_to_all | solution.py:265
  115.4 29.5 %attend_all.1 = (bf16[256,2048]{1,0:T(8,128)(2,1)}, bf16[16,128,896]{2,1,0:T(8,128)(2,1)}) custom-call(s32[8]{0:T(128)} %multiply_add_fusion.1.slot_ref, bf16[16,64,896]{2,1,0:T(8,128)(2,1)} %all-to-all-done.x_ref, bf16[512,2048]{1,0:T(8,128)(2,1)} %get-tuple-element.9.ka_ref, bf16[512,2048]{1,0:T(8,128)(2,1)} %get-tuple-element.10.va_ref, ...), custom_call_target="tpu_custom_call" | custom-call | flops 12616466432 | bytes 19922944 | tf_op jit(solution)/shard_map/attend_all/pallas_call | solution.py:203
  144.9 0.0 copy-start.1
  144.9 7.5 %all-to-all-start.2 = ((bf16[16,128,896]{2,1,0:T(8,128)(2,1)}), bf16[16,128,896]{2,1,0:T(8,128)(2,1)}, u32[]{:S(2)}, u32[]{:S(2)}) async-start(bf16[16,128,896]{2,1,0:T(8,128)(2,1)} %get-tuple-element.13), calls=%async_computation.2 | async-start | bytes 7340032 | tf_op jit(solution)/shard_map/all_to_all | solution.py:265
  152.4 0.0 copy-done.1
  152.4 0.1 slice.42
  152.5 3.1 %collective-permute-start.1 = (bf16[63,2048]{1,0:T(8,128)(2,1)S(1)}, bf16[63,2048]{1,0:T(8,128)(2,1)S(1)}, u32[]{:S(2)}, u32[]{:S(2)}) collective-permute-start(bf16[63,2048]{1,0:T(8,128)(2,1)S(1)} %slice.42), channel_id=1, source_target_pairs={{0,1},{1,2},{2,3},{3,4},{4,5},{5,6},{6,7},{7,8},{8,9},{9,10},{10,1... | collective-permute-start | bytes 774152 | tf_op jit(solution)/shard_map/ppermute | solution.py:26
  155.6 0.1 slice.43
  155.6 83.6 %collective-permute-done.1 = bf16[63,2048]{1,0:T(8,128)(2,1)S(1)} collective-permute-done((bf16[63,2048]{1,0:T(8,128)(2,1)S(1)}, bf16[63,2048]{1,0:T(8,128)(2,1)S(1)}, u32[]{:S(2)}, u32[]{:S(2)}) %collective-permute-start.1) | collective-permute-done | bytes 258080 | tf_op jit(solution)/shard_map/ppermute | solution.py:26
  239.2 1.2 pad_maximum_fusion.2
  240.5 0.0 all-to-all-done.2.x_ref
  240.5 4.7 %place.1 = bf16[8,128,896]{2,1,0:T(8,128)(2,1)} custom-call(s32[8]{0:T(128)} %multiply_add_fusion.slot_ref, bf16[16,128,896]{2,1,0:T(8,128)(2,1)} %all-to-all-done.2.x_ref), custom_call_target="tpu_custom_call" | custom-call | tf_op jit(solution)/shard_map/place/pallas_call | solution.py:251
  (5 shorter events, 0.1 us)
Async XLA Ops:
  0.6 7.2 %copy-start.5 = (s32[8]{0:T(128)S(1)}, s32[8]{0:T(128)}, u32[]{:S(2)}) copy-start(s32[8]{0:T(128)} %param.14) | copy-start | bytes 100
  4.8 14.7 %collective-permute-start = (bf16[128,2048]{1,0:T(8,128)(2,1)S(1)}, bf16[128,2048]{1,0:T(8,128)(2,1)S(1)}, u32[]{:S(2)}, u32[]{:S(2)}) collective-permute-start(bf16[128,2048]{1,0:T(8,128)(2,1)S(1)} %maximum_maximum_fusion), channel_id=1, source_target_pairs={{1,0},{2,1},{3,2},{4,3},{5,4},{6,5},{7,6},{8,7},{9,8},{10,9},{11,1... | collective-permute-start | bytes 1572872 | tf_op jit(solution)/shard_map/ppermute | solution.py:26
  19.6 19.6 %copy-start.2 = (bf16[128,2048]{1,0:T(8,128)(2,1)}, bf16[128,2048]{1,0:T(8,128)(2,1)S(1)}, u32[]{:S(2)}) copy-start(bf16[128,2048]{1,0:T(8,128)(2,1)S(1)} %collective-permute-done) | copy-start | bytes 1572868
  19.6 48.5 %all-to-all-start.1 = ((bf16[16,64,896]{2,1,0:T(8,128)(2,1)}), bf16[16,64,896]{2,1,0:T(8,128)(2,1)S(1)}, u32[]{:S(2)}, u32[]{:S(2)}) async-start(bf16[16,64,896]{2,1,0:T(8,128)(2,1)} %encode_part.3), calls=%async_computation.1 | async-start | bytes 3670016 | tf_op jit(solution)/shard_map/all_to_all | solution.py:265
  68.1 8.3 %copy-start = (bf16[16,64,896]{2,1,0:T(8,128)(2,1)}, bf16[16,64,896]{2,1,0:T(8,128)(2,1)S(1)}, u32[]{:S(2)}) copy-start(bf16[16,64,896]{2,1,0:T(8,128)(2,1)S(1)} %all-to-all-done.1.x_ref) | copy-start | bytes 5505028
  68.1 47.3 %all-to-all-start = ((bf16[16,64,896]{2,1,0:T(8,128)(2,1)}), bf16[16,64,896]{2,1,0:T(8,128)(2,1)}, u32[]{:S(2)}, u32[]{:S(2)}) async-start(bf16[16,64,896]{2,1,0:T(8,128)(2,1)} %encode_part.2), calls=%async_computation | async-start | bytes 3670016 | tf_op jit(solution)/shard_map/all_to_all | solution.py:265
  75.0 2.7 %copy-start.3 = (s32[4]{0:T(128)S(1)}, s32[4]{0:T(128)}, u32[]{:S(2)}) copy-start(s32[4]{0:T(128)} %param.15) | copy-start | bytes 52
  75.0 2.8 %copy-start.4 = (s32[4,2]{0,1:T(2,128)S(1)}, s32[4,2]{0,1:T(2,128)}, u32[]{:S(2)}) copy-start(s32[4,2]{0,1:T(2,128)} %param.13) | copy-start | bytes 100
  144.9 7.5 %copy-start.1 = (bf16[256,2048]{1,0:T(8,128)(2,1)S(1)}, bf16[256,2048]{1,0:T(8,128)(2,1)}, u32[]{:S(2)}) copy-start(bf16[256,2048]{1,0:T(8,128)(2,1)} %get-tuple-element.12) | copy-start | bytes 3145732
  144.9 95.5 %all-to-all-start.2 = ((bf16[16,128,896]{2,1,0:T(8,128)(2,1)}), bf16[16,128,896]{2,1,0:T(8,128)(2,1)}, u32[]{:S(2)}, u32[]{:S(2)}) async-start(bf16[16,128,896]{2,1,0:T(8,128)(2,1)} %get-tuple-element.13), calls=%async_computation.2 | async-start | bytes 7340032 | tf_op jit(solution)/shard_map/all_to_all | solution.py:265
  152.5 86.8 %collective-permute-start.1 = (bf16[63,2048]{1,0:T(8,128)(2,1)S(1)}, bf16[63,2048]{1,0:T(8,128)(2,1)S(1)}, u32[]{:S(2)}, u32[]{:S(2)}) collective-permute-start(bf16[63,2048]{1,0:T(8,128)(2,1)S(1)} %slice.42), channel_id=1, source_target_pairs={{0,1},{1,2},{2,3},{3,4},{4,5},{5,6},{6,7},{7,8},{8,9},{9,10},{10,1... | collective-permute-start | bytes 774152 | tf_op jit(solution)/shard_map/ppermute | solution.py:26

commit v6 on v5

--- a/solution.py
+++ b/solution.py
@@ -10,7 +10,7 @@
 
 HEAD_DIM = 128
 CAP = 2
-CHUNK = 256
+CHUNK = 512
 PARTS = 2
 
 
@@ -100,7 +100,7 @@
     slot_total, rows, width = incoming.shape
     slots = recv_slot.shape[0]
     features = key_weight.shape[1]
-    wide = 2 * CHUNK
+    wide = CHUNK
     weight = pl.BlockSpec((width, wide), lambda j, s: (0, j))
     result = pl.BlockSpec((slots * rows, wide), lambda j, s: (0, j))
     shape = jax.ShapeDtypeStruct((slots * rows, features), jnp.bfloat16)

time: 246 us -> 245 us (level)
  no operation moved by 1% of the time
where the time goes in v6:
time: 245 us; the launch traced here: 244 us
  waiting for transfers between devices  136 us (56%)
  Pallas kernels  60.4 us (25%)
  starting transfers between devices  31 us (13%)
  local copies, waits for them, and re-layouts  8.26 us (3%)
  other arithmetic  5.28 us (2%)
  between operations  2.73 us (1%)
    ppermute x2, waiting for transfers between devices, from_behind(): return lax.ppermute(block, axis, route)  85.5 us
    all_to_all x3, waiting for transfers between devices, exchange(): return lax.all_to_all(block, 'nbr', split_axis=0, concat_axis=0, tiled=True)  50.6 us
    pallas_call x1, Pallas kernels, attend_all(): pl.pallas_call(functools.partial(attend_kernel, slots, spans), grid_spec=...  28.1 us
    all_to_all x3, starting transfers between devices, exchange(): return lax.all_to_all(block, 'nbr', split_axis=0, concat_axis=0, tiled=True)  24.9 us
    pallas_call x2, Pallas kernels, encode_part(): pl.pallas_call(encode_kernel, grid_spec=pltpu.PrefetchScalarGridSpec(num_...  18.1 us
    pallas_call x1, Pallas kernels, project_part(): pl.pallas_call(functools.partial(project_kernel, slots), grid_spec=pltpu....  9.54 us
    ppermute x2, starting transfers between devices, from_behind(): return lax.ppermute(block, axis, route)  6.1 us
  transfers between devices with their start and end apart: 5, of which 4 were waited for; matrix products, arithmetic and copies ran while one was open for 5% of the time, Pallas kernels for 11%

profile of v6, /device:TPU:17, one launch (start us, length us, event | category | flops | bytes accessed | tf_op | source)
XLA Modules:
  0.0 243.8 jit_solution(17935075587443028851)
XLA Ops:
  0.6 0.0 copy-start.5
  2.6 1.0 slice.33
  3.6 1.0 slice.34
  4.6 0.1 pad.10.clone
  4.6 0.2 maximum_maximum_fusion
  4.8 3.0 %collective-permute-start = (bf16[128,2048]{1,0:T(8,128)(2,1)S(1)}, bf16[128,2048]{1,0:T(8,128)(2,1)S(1)}, u32[]{:S(2)}, u32[]{:S(2)}) collective-permute-start(bf16[128,2048]{1,0:T(8,128)(2,1)S(1)} %maximum_maximum_fusion), channel_id=1, source_target_pairs={{1,0},{2,1},{3,2},{4,3},{5,4},{6,5},{7,6},{8,7},{9,8},{10,9},{11,1... | collective-permute-start | bytes 1572872 | tf_op jit(solution)/shard_map/ppermute | solution.py:26
  7.9 0.0 copy-done.5
  7.9 0.2 convert_reduce_fusion
  8.1 0.5 multiply_add_fusion.slot_ref
  8.6 9.1 %encode_part.3 = bf16[16,64,896]{2,1,0:T(8,128)(2,1)} custom-call(s32[8]{0:T(128)} %multiply_add_fusion.slot_ref, bf16[8,128,896]{2,1,0:T(8,128)(2,1)} %x_ref.3, bf16[896,1792]{1,0:T(8,128)(2,1)} %in_ref.3, bf16[1792,896]{1,0:T(8,128)(2,1)} %out_w_ref.3), custom_call_target="tpu_custom_call" | custom-call | flops 3288334336 | bytes 9175040 | tf_op jit(solution)/shard_map/encode_part/pallas_call | solution.py:58
  17.7 1.9 collective-permute-done
  19.6 0.0 copy-start.2
  19.6 10.5 %all-to-all-start.1 = ((bf16[16,64,896]{2,1,0:T(8,128)(2,1)}), bf16[16,64,896]{2,1,0:T(8,128)(2,1)S(1)}, u32[]{:S(2)}, u32[]{:S(2)}) async-start(bf16[16,64,896]{2,1,0:T(8,128)(2,1)} %encode_part.3), calls=%async_computation.1 | async-start | bytes 3670016 | tf_op jit(solution)/shard_map/all_to_all | solution.py:265
  30.1 9.0 %encode_part.2 = bf16[16,64,896]{2,1,0:T(8,128)(2,1)} custom-call(s32[8]{0:T(128)} %multiply_add_fusion.slot_ref, bf16[8,128,896]{2,1,0:T(8,128)(2,1)} %x_ref.3, bf16[896,1792]{1,0:T(8,128)(2,1)} %in_ref.3, bf16[1792,896]{1,0:T(8,128)(2,1)} %out_w_ref.3), custom_call_target="tpu_custom_call" | custom-call | flops 3288334336 | bytes 9175040 | tf_op jit(solution)/shard_map/encode_part/pallas_call | solution.py:58
  39.1 0.0 copy-done.2
  39.1 29.0 %all-to-all-done.1.x_ref = bf16[16,64,896]{2,1,0:T(8,128)(2,1)S(1)} async-done(((bf16[16,64,896]{2,1,0:T(8,128)(2,1)}), bf16[16,64,896]{2,1,0:T(8,128)(2,1)S(1)}, u32[]{:S(2)}, u32[]{:S(2)}) %all-to-all-start.1) | async-done | bytes 1835040 | tf_op jit(solution)/shard_map/all_to_all | solution.py:265
  68.1 0.0 copy-start
  68.1 6.9 %all-to-all-start = ((bf16[16,64,896]{2,1,0:T(8,128)(2,1)}), bf16[16,64,896]{2,1,0:T(8,128)(2,1)}, u32[]{:S(2)}, u32[]{:S(2)}) async-start(bf16[16,64,896]{2,1,0:T(8,128)(2,1)} %encode_part.2), calls=%async_computation | async-start | bytes 3670016 | tf_op jit(solution)/shard_map/all_to_all | solution.py:265
  75.0 0.0 copy-start.3
  75.0 0.0 copy-start.4
  75.0 1.4 slice.36
  76.4 0.0 copy-done
  76.4 1.3 slice.38
  77.7 0.0 copy-done.3
  77.8 0.1 slice.40
  77.8 0.0 copy-done.4
  77.8 0.1 copy.15
  77.9 0.1 reshape.133
  78.0 0.2 convert_reduce_fusion.1
  78.2 0.5 multiply_add_fusion.1.slot_ref
  78.8 1.3 slice.41
  80.0 0.7 maximum_compare_fusion
  80.7 0.1 or_convert_fusion
  80.8 0.8 reshape.135.valid_ref
  81.6 1.1 fusion.6
  82.7 1.6 pad_maximum_fusion
  84.3 9.5 %project_part.1 = (bf16[512,2048]{1,0:T(8,128)(2,1)}, bf16[512,2048]{1,0:T(8,128)(2,1)}) custom-call(s32[8]{0:T(128)} %multiply_add_fusion.1.slot_ref, bf16[16,64,896]{2,1,0:T(8,128)(2,1)} %copy-done, bf16[896,2048]{1,0:T(8,128)(2,1)} %kw_ref.3, bf16[896,2048]{1,0:T(8,128)(2,1)} %vw_ref.3), custom_call_target="tpu_custom_call" | custom-call | flops 3758096384 | bytes 11534336 | tf_op jit(solution)/shard_map/project_part/pallas_call | solution.py:107
  93.8 21.6 %all-to-all-done.x_ref = bf16[16,64,896]{2,1,0:T(8,128)(2,1)} async-done(((bf16[16,64,896]{2,1,0:T(8,128)(2,1)}), bf16[16,64,896]{2,1,0:T(8,128)(2,1)}, u32[]{:S(2)}, u32[]{:S(2)}) %all-to-all-start) | async-done | bytes 1835040 | tf_op jit(solution)/shard_map/all_to_all | solution.py:265
  115.4 28.1 %attend_all.1 = (bf16[256,2048]{1,0:T(8,128)(2,1)}, bf16[16,128,896]{2,1,0:T(8,128)(2,1)}) custom-call(s32[8]{0:T(128)} %multiply_add_fusion.1.slot_ref, bf16[16,64,896]{2,1,0:T(8,128)(2,1)} %all-to-all-done.x_ref, bf16[512,2048]{1,0:T(8,128)(2,1)} %get-tuple-element.9.ka_ref, bf16[512,2048]{1,0:T(8,128)(2,1)} %get-tuple-element.10.va_ref, ...), custom_call_target="tpu_custom_call" | custom-call | flops 12616466432 | bytes 19922944 | tf_op jit(solution)/shard_map/attend_all/pallas_call | solution.py:203
  143.5 0.0 copy-start.1
  143.5 7.5 %all-to-all-start.2 = ((bf16[16,128,896]{2,1,0:T(8,128)(2,1)}), bf16[16,128,896]{2,1,0:T(8,128)(2,1)}, u32[]{:S(2)}, u32[]{:S(2)}) async-start(bf16[16,128,896]{2,1,0:T(8,128)(2,1)} %get-tuple-element.13), calls=%async_computation.2 | async-start | bytes 7340032 | tf_op jit(solution)/shard_map/all_to_all | solution.py:265
  151.0 0.0 copy-done.1
  151.0 0.1 slice.42
  151.1 3.1 %collective-permute-start.1 = (bf16[63,2048]{1,0:T(8,128)(2,1)S(1)}, bf16[63,2048]{1,0:T(8,128)(2,1)S(1)}, u32[]{:S(2)}, u32[]{:S(2)}) collective-permute-start(bf16[63,2048]{1,0:T(8,128)(2,1)S(1)} %slice.42), channel_id=1, source_target_pairs={{0,1},{1,2},{2,3},{3,4},{4,5},{5,6},{6,7},{7,8},{8,9},{9,10},{10,1... | collective-permute-start | bytes 774152 | tf_op jit(solution)/shard_map/ppermute | solution.py:26
  154.2 0.1 slice.43
  154.2 83.6 %collective-permute-done.1 = bf16[63,2048]{1,0:T(8,128)(2,1)S(1)} collective-permute-done((bf16[63,2048]{1,0:T(8,128)(2,1)S(1)}, bf16[63,2048]{1,0:T(8,128)(2,1)S(1)}, u32[]{:S(2)}, u32[]{:S(2)}) %collective-permute-start.1) | collective-permute-done | bytes 258080 | tf_op jit(solution)/shard_map/ppermute | solution.py:26
  237.8 1.2 pad_maximum_fusion.2
  239.1 0.0 all-to-all-done.2.x_ref
  239.1 4.7 %place.1 = bf16[8,128,896]{2,1,0:T(8,128)(2,1)} custom-call(s32[8]{0:T(128)} %multiply_add_fusion.slot_ref, bf16[16,128,896]{2,1,0:T(8,128)(2,1)} %all-to-all-done.2.x_ref), custom_call_target="tpu_custom_call" | custom-call | tf_op jit(solution)/shard_map/place/pallas_call | solution.py:251
  (5 shorter events, 0.1 us)
Async XLA Ops:
  0.6 7.2 %copy-start.5 = (s32[8]{0:T(128)S(1)}, s32[8]{0:T(128)}, u32[]{:S(2)}) copy-start(s32[8]{0:T(128)} %param.14) | copy-start | bytes 100
  4.8 14.7 %collective-permute-start = (bf16[128,2048]{1,0:T(8,128)(2,1)S(1)}, bf16[128,2048]{1,0:T(8,128)(2,1)S(1)}, u32[]{:S(2)}, u32[]{:S(2)}) collective-permute-start(bf16[128,2048]{1,0:T(8,128)(2,1)S(1)} %maximum_maximum_fusion), channel_id=1, source_target_pairs={{1,0},{2,1},{3,2},{4,3},{5,4},{6,5},{7,6},{8,7},{9,8},{10,9},{11,1... | collective-permute-start | bytes 1572872 | tf_op jit(solution)/shard_map/ppermute | solution.py:26
  19.6 19.6 %copy-start.2 = (bf16[128,2048]{1,0:T(8,128)(2,1)}, bf16[128,2048]{1,0:T(8,128)(2,1)S(1)}, u32[]{:S(2)}) copy-start(bf16[128,2048]{1,0:T(8,128)(2,1)S(1)} %collective-permute-done) | copy-start | bytes 1572868
  19.6 48.5 %all-to-all-start.1 = ((bf16[16,64,896]{2,1,0:T(8,128)(2,1)}), bf16[16,64,896]{2,1,0:T(8,128)(2,1)S(1)}, u32[]{:S(2)}, u32[]{:S(2)}) async-start(bf16[16,64,896]{2,1,0:T(8,128)(2,1)} %encode_part.3), calls=%async_computation.1 | async-start | bytes 3670016 | tf_op jit(solution)/shard_map/all_to_all | solution.py:265
  68.1 8.3 %copy-start = (bf16[16,64,896]{2,1,0:T(8,128)(2,1)}, bf16[16,64,896]{2,1,0:T(8,128)(2,1)S(1)}, u32[]{:S(2)}) copy-start(bf16[16,64,896]{2,1,0:T(8,128)(2,1)S(1)} %all-to-all-done.1.x_ref) | copy-start | bytes 5505028
  68.1 47.3 %all-to-all-start = ((bf16[16,64,896]{2,1,0:T(8,128)(2,1)}), bf16[16,64,896]{2,1,0:T(8,128)(2,1)}, u32[]{:S(2)}, u32[]{:S(2)}) async-start(bf16[16,64,896]{2,1,0:T(8,128)(2,1)} %encode_part.2), calls=%async_computation | async-start | bytes 3670016 | tf_op jit(solution)/shard_map/all_to_all | solution.py:265
  75.0 2.7 %copy-start.3 = (s32[4]{0:T(128)S(1)}, s32[4]{0:T(128)}, u32[]{:S(2)}) copy-start(s32[4]{0:T(128)} %param.15) | copy-start | bytes 52
  75.0 2.8 %copy-start.4 = (s32[4,2]{0,1:T(2,128)S(1)}, s32[4,2]{0,1:T(2,128)}, u32[]{:S(2)}) copy-start(s32[4,2]{0,1:T(2,128)} %param.13) | copy-start | bytes 100
  143.5 7.5 %copy-start.1 = (bf16[256,2048]{1,0:T(8,128)(2,1)S(1)}, bf16[256,2048]{1,0:T(8,128)(2,1)}, u32[]{:S(2)}) copy-start(bf16[256,2048]{1,0:T(8,128)(2,1)} %get-tuple-element.12) | copy-start | bytes 3145732
  143.5 95.5 %all-to-all-start.2 = ((bf16[16,128,896]{2,1,0:T(8,128)(2,1)}), bf16[16,128,896]{2,1,0:T(8,128)(2,1)}, u32[]{:S(2)}, u32[]{:S(2)}) async-start(bf16[16,128,896]{2,1,0:T(8,128)(2,1)} %get-tuple-element.13), calls=%async_computation.2 | async-start | bytes 7340032 | tf_op jit(solution)/shard_map/all_to_all | solution.py:265
  151.1 86.8 %collective-permute-start.1 = (bf16[63,2048]{1,0:T(8,128)(2,1)S(1)}, bf16[63,2048]{1,0:T(8,128)(2,1)S(1)}, u32[]{:S(2)}, u32[]{:S(2)}) collective-permute-start(bf16[63,2048]{1,0:T(8,128)(2,1)S(1)} %slice.42), channel_id=1, source_target_pairs={{0,1},{1,2},{2,3},{3,4},{4,5},{5,6},{6,7},{7,8},{8,9},{9,10},{10,1... | collective-permute-start | bytes 774152 | tf_op jit(solution)/shard_map/ppermute | solution.py:26
